TPU v7x, 32 devices: a whole 2x2x4 slice. The times are simulated.
32 devices in a mesh: shard: 16 (over z, x, core), replica: 2 (over y).
Axes of the slice: x: 2, y: 2, z: 4, core: 2. Of those that a mesh axis runs over, the one named last changes fastest.
Arguments:
- tokens: float32 [4096, 1024], P(('shard', 'replica')), may hold values from -6 to 6
- segment_ids: int32 [32, 128], P(('shard', 'replica')), may hold values from 0 to 3, never falling along the last dimension, each value on 1 to 64 neighbouring positions
- cotangent: float32 [4096, 1024], P(('shard', 'replica')), may hold values from -6 to 6
- norm1_gain: bfloat16 [1024], P('shard'), may hold values from 0.099609375 to 1.8984375
- norm1_shift: bfloat16 [1024], P('shard'), may hold values from -3 to 3
- qkv_weight: bfloat16 [1024, 3072], P('shard'), may hold values from -0.1875 to 0.1875
- query_bias: bfloat16 [1024], P('shard'), may hold values from -3 to 3
- value_bias: bfloat16 [1024], P('shard'), may hold values from -3 to 3
- out_weight: bfloat16 [1024, 1024], P('shard'), may hold values from -0.75 to 0.75
- out_bias: bfloat16 [1024], P('shard'), may hold values from -3 to 3
- norm2_gain: bfloat16 [1024], P('shard'), may hold values from 0.099609375 to 1.8984375
- norm2_shift: bfloat16 [1024], P('shard'), may hold values from -3 to 3
- fc_weight: bfloat16 [1024, 4096], P('shard'), may hold values from -0.1875 to 0.1875
- fc_bias: bfloat16 [4096], P('shard'), may hold values from -3 to 3
- proj_weight: bfloat16 [4096, 1024], P('shard'), may hold values from -0.09375 to 0.09375
- proj_bias: bfloat16 [1024], P('shard'), may hold values from -3 to 3
Outputs:
- output: float32 [4096, 1024], P(('shard', 'replica'))
- tokens_grad: float32 [4096, 1024], P(('shard', 'replica'))
- norm1_gain_grad: float32 [1024], P('shard')
- norm1_shift_grad: float32 [1024], P('shard')
- qkv_weight_grad: float32 [1024, 3072], P('shard')
- query_bias_grad: float32 [1024], P('shard')
- value_bias_grad: float32 [1024], P('shard')
- out_weight_grad: float32 [1024, 1024], P('shard')
- out_bias_grad: float32 [1024], P('shard')
- norm2_gain_grad: float32 [1024], P('shard')
- norm2_shift_grad: float32 [1024], P('shard')
- fc_weight_grad: float32 [1024, 4096], P('shard')
- fc_bias_grad: float32 [4096], P('shard')
- proj_weight_grad: float32 [4096, 1024], P('shard')
- proj_bias_grad: float32 [1024], P('shard')
Inputs may be any that keep to these rules, and one draw needn't show every extreme that they name: `segment_ids`: in each row (one device's tokens) the numbers never fall, every number from 0 to 3 occurs as one run of 1 to 64 positions, and one run holds exactly 64.
All inputs are finite; a program needn't handle non-finite values.
Results may differ from a plain program's by a relative error of at most 0.012.
Values may be sent and summed in bfloat16 or wider, within the bound.
A program may use at most 192 MiB of HBM per device.

v0:
```python
import jax
import jax.numpy as jnp
from jax import lax
from jax.sharding import PartitionSpec as P

HEADS = 16
HEAD = 64


EPS = 1e-05
GELU_C = 0.7978845608028654
GELU_A = 0.044715


def layer_norm(values, gain, shift):
    row_mean = jnp.mean(values, axis=-1, keepdims=True)
    centered = values - row_mean
    inv_std = lax.rsqrt(jnp.mean(centered * centered, axis=-1, keepdims=True) + EPS)
    normed = centered * inv_std
    return (normed * gain.astype(jnp.float32) + shift.astype(jnp.float32), normed, inv_std)


def norm_back(grad_out, normed, inv_std, gain):
    scaled = grad_out * gain.astype(jnp.float32)
    return inv_std * (
        scaled
        - jnp.mean(scaled, axis=-1, keepdims=True)
        - normed * jnp.mean(scaled * normed, axis=-1, keepdims=True)
    )


def gelu_pair(pre_act):
    tangent = jnp.tanh(GELU_C * (pre_act + GELU_A * pre_act * pre_act * pre_act))
    value = 0.5 * pre_act * (1.0 + tangent)
    slope = 0.5 * (1.0 + tangent) + 0.5 * pre_act * (1.0 - tangent * tangent) * GELU_C * (
        1.0 + 3.0 * GELU_A * pre_act * pre_act
    )
    return (value, slope)


def contract(left, right, left_axis, right_axis):
    return lax.dot_general(
        left, right, (((left_axis,), (right_axis,)), ((), ())), preferred_element_type=jnp.float32
    )


def masked_scores(query, keyed, segment_row, scale):
    rows = query.shape[0]
    scores = jnp.einsum("qhd,khd->hqk", query, keyed, preferred_element_type=jnp.float32) * scale
    position = jnp.arange(rows)
    allowed = (segment_row[:, None] == segment_row[None, :]) & (
        position[None, :] <= position[:, None]
    )
    return jnp.where(allowed[None], scores, -1e30)


def on_device(
    tokens,
    segment_ids,
    cotangent,
    norm1_gain,
    norm1_shift,
    qkv_weight,
    query_bias,
    value_bias,
    out_weight,
    out_bias,
    norm2_gain,
    norm2_shift,
    fc_weight,
    fc_bias,
    proj_weight,
    proj_bias,
):
    rows, width = tokens.shape
    segment_row = segment_ids[0]
    scale = HEAD ** (-0.5)
    gain1, shift1, w_qkv, bias_query, bias_value, w_out, bias_out = (
        lax.all_gather(norm1_gain, "shard", axis=0, tiled=True),
        lax.all_gather(norm1_shift, "shard", axis=0, tiled=True),
        lax.all_gather(qkv_weight, "shard", axis=0, tiled=True),
        lax.all_gather(query_bias, "shard", axis=0, tiled=True),
        lax.all_gather(value_bias, "shard", axis=0, tiled=True),
        lax.all_gather(out_weight, "shard", axis=0, tiled=True),
        lax.all_gather(out_bias, "shard", axis=0, tiled=True),
    )
    ln1, normed1, inv1 = layer_norm(tokens, gain1, shift1)
    input1 = ln1.astype(jnp.bfloat16)
    qkv_bias = jnp.concatenate(
        [
            bias_query.astype(jnp.float32),
            jnp.zeros((width,), jnp.float32),
            bias_value.astype(jnp.float32),
        ]
    )
    projected = jnp.dot(input1, w_qkv, preferred_element_type=jnp.float32) + qkv_bias
    query = projected[:, :width].reshape(rows, HEADS, HEAD).astype(jnp.bfloat16)
    keyed = projected[:, width : 2 * width].reshape(rows, HEADS, HEAD).astype(jnp.bfloat16)
    valued = projected[:, 2 * width :].reshape(rows, HEADS, HEAD).astype(jnp.bfloat16)
    scores = masked_scores(query, keyed, segment_row, scale)
    top = jnp.max(scores, axis=-1, keepdims=True)
    log_total = top + jnp.log(jnp.sum(jnp.exp(scores - top), axis=-1, keepdims=True))
    probs_low = jnp.exp(scores - log_total).astype(jnp.bfloat16)
    context = jnp.einsum("hqk,khd->qhd", probs_low, valued, preferred_element_type=jnp.float32)
    context = context.reshape(rows, width).astype(jnp.bfloat16)
    middle = (
        tokens
        + jnp.dot(context, w_out, preferred_element_type=jnp.float32)
        + bias_out.astype(jnp.float32)
    )
    gain2, shift2, w_fc, bias_fc, w_proj, bias_proj = (
        lax.all_gather(norm2_gain, "shard", axis=0, tiled=True),
        lax.all_gather(norm2_shift, "shard", axis=0, tiled=True),
        lax.all_gather(fc_weight, "shard", axis=0, tiled=True),
        lax.all_gather(fc_bias, "shard", axis=0, tiled=True),
        lax.all_gather(proj_weight, "shard", axis=0, tiled=True),
        lax.all_gather(proj_bias, "shard", axis=0, tiled=True),
    )
    ln2, normed2, inv2 = layer_norm(middle, gain2, shift2)
    input2 = ln2.astype(jnp.bfloat16)
    pre_act = jnp.dot(input2, w_fc, preferred_element_type=jnp.float32) + bias_fc.astype(
        jnp.float32
    )
    gelu_value, gelu_slope = gelu_pair(pre_act)
    activated = gelu_value.astype(jnp.bfloat16)
    output = (
        middle
        + jnp.dot(activated, w_proj, preferred_element_type=jnp.float32)
        + bias_proj.astype(jnp.float32)
    )
    grad_proj_bias = jnp.sum(cotangent, axis=0)
    cot_low = cotangent.astype(jnp.bfloat16)
    grad_pre = contract(cot_low, w_proj, 1, 1) * gelu_slope
    grad_fc_bias = jnp.sum(grad_pre, axis=0)
    grad_pre_low = grad_pre.astype(jnp.bfloat16)
    grad_fc_weight = contract(input2, grad_pre_low, 0, 0)
    grad_in2 = contract(grad_pre_low, w_fc, 1, 1)
    grad_gain2 = jnp.sum(grad_in2 * normed2, axis=0)
    grad_shift2 = jnp.sum(grad_in2, axis=0)
    grad_middle = cotangent + norm_back(grad_in2, normed2, inv2, gain2)
    grad_proj_weight = contract(activated, cot_low, 0, 0)
    (
        share_gain2,
        share_shift2,
        share_fc_weight,
        share_fc_bias,
        share_proj_weight,
        share_proj_bias,
    ) = (
        lax.psum_scatter(grad_gain2, "shard", scatter_dimension=0, tiled=True),
        lax.psum_scatter(grad_shift2, "shard", scatter_dimension=0, tiled=True),
        lax.psum_scatter(grad_fc_weight, "shard", scatter_dimension=0, tiled=True),
        lax.psum_scatter(grad_fc_bias, "shard", scatter_dimension=0, tiled=True),
        lax.psum_scatter(grad_proj_weight, "shard", scatter_dimension=0, tiled=True),
        lax.psum_scatter(grad_proj_bias, "shard", scatter_dimension=0, tiled=True),
    )
    (
        share_gain2,
        share_shift2,
        share_fc_weight,
        share_fc_bias,
        share_proj_weight,
        share_proj_bias,
    ) = lax.psum(
        (
            share_gain2,
            share_shift2,
            share_fc_weight,
            share_fc_bias,
            share_proj_weight,
            share_proj_bias,
        ),
        "replica",
    )
    grad_out_bias = jnp.sum(grad_middle, axis=0)
    mid_low = grad_middle.astype(jnp.bfloat16)
    grad_out_weight = contract(context, mid_low, 0, 0)
    grad_context = contract(mid_low, w_out, 1, 1)
    grad_context = grad_context.reshape(rows, HEADS, HEAD).astype(jnp.bfloat16)
    again_scores = masked_scores(query, keyed, segment_row, scale)
    probs = jnp.exp(again_scores - log_total)
    probs_low = probs.astype(jnp.bfloat16)
    grad_value = jnp.einsum(
        "hqk,qhd->khd", probs_low, grad_context, preferred_element_type=jnp.float32
    )
    grad_probs = jnp.einsum(
        "qhd,khd->hqk", grad_context, valued, preferred_element_type=jnp.float32
    )
    grad_scores = probs * (grad_probs - jnp.sum(probs * grad_probs, axis=-1, keepdims=True)) * scale
    grad_scores = grad_scores.astype(jnp.bfloat16)
    grad_query = jnp.einsum("hqk,khd->qhd", grad_scores, keyed, preferred_element_type=jnp.float32)
    grad_key = jnp.einsum("hqk,qhd->khd", grad_scores, query, preferred_element_type=jnp.float32)
    grad_query = grad_query.reshape(rows, width)
    grad_key = grad_key.reshape(rows, width)
    grad_value = grad_value.reshape(rows, width)
    grad_query_bias = jnp.sum(grad_query, axis=0)
    grad_value_bias = jnp.sum(grad_value, axis=0)
    grad_qkv = jnp.concatenate([grad_query, grad_key, grad_value], axis=1).astype(jnp.bfloat16)
    grad_qkv_weight = contract(input1, grad_qkv, 0, 0)
    grad_in1 = contract(grad_qkv, w_qkv, 1, 1)
    grad_gain1 = jnp.sum(grad_in1 * normed1, axis=0)
    grad_shift1 = jnp.sum(grad_in1, axis=0)
    tokens_grad = grad_middle + norm_back(grad_in1, normed1, inv1, gain1)
    (
        share_gain1,
        share_shift1,
        share_qkv_weight,
        share_query_bias,
        share_value_bias,
        share_out_weight,
        share_out_bias,
    ) = (
        lax.psum_scatter(grad_gain1, "shard", scatter_dimension=0, tiled=True),
        lax.psum_scatter(grad_shift1, "shard", scatter_dimension=0, tiled=True),
        lax.psum_scatter(grad_qkv_weight, "shard", scatter_dimension=0, tiled=True),
        lax.psum_scatter(grad_query_bias, "shard", scatter_dimension=0, tiled=True),
        lax.psum_scatter(grad_value_bias, "shard", scatter_dimension=0, tiled=True),
        lax.psum_scatter(grad_out_weight, "shard", scatter_dimension=0, tiled=True),
        lax.psum_scatter(grad_out_bias, "shard", scatter_dimension=0, tiled=True),
    )
    (
        share_gain1,
        share_shift1,
        share_qkv_weight,
        share_query_bias,
        share_value_bias,
        share_out_weight,
        share_out_bias,
    ) = lax.psum(
        (
            share_gain1,
            share_shift1,
            share_qkv_weight,
            share_query_bias,
            share_value_bias,
            share_out_weight,
            share_out_bias,
        ),
        "replica",
    )
    return (
        output,
        tokens_grad,
        share_gain1,
        share_shift1,
        share_qkv_weight,
        share_query_bias,
        share_value_bias,
        share_out_weight,
        share_out_bias,
        share_gain2,
        share_shift2,
        share_fc_weight,
        share_fc_bias,
        share_proj_weight,
        share_proj_bias,
    )


def solution(mesh):
    in_specs = (
        P(("shard", "replica"), None),
        P(("shard", "replica"), None),
        P(("shard", "replica"), None),
        P("shard"),
        P("shard"),
        P("shard", None),
        P("shard"),
        P("shard"),
        P("shard", None),
        P("shard"),
        P("shard"),
        P("shard"),
        P("shard", None),
        P("shard"),
        P("shard", None),
        P("shard"),
    )
    out_specs = (
        P(("shard", "replica"), None),
        P(("shard", "replica"), None),
        P("shard"),
        P("shard"),
        P("shard", None),
        P("shard"),
        P("shard"),
        P("shard", None),
        P("shard"),
        P("shard"),
        P("shard"),
        P("shard", None),
        P("shard"),
        P("shard", None),
        P("shard"),
    )
    return jax.shard_map(
        on_device, mesh=mesh, in_specs=in_specs, out_specs=out_specs, check_vma=False
    )
```

profile of v0, /device:TPU:0, one launch (start us, length us, event | category | flops | bytes accessed | tf_op | source)
XLA Modules:
  0.0 957.4 jit_solution(4036300594005818929)
XLA Ops:
  10.0 1.3 fusion.50
  18.7 64.0 %all-reduce.20 = (bf16[1024]{0:T(1024)(128)(2,1)S(1)}, bf16[1024]{0:T(1024)(128)(2,1)S(1)}, bf16[1024]{0:T(1024)(128)(2,1)S(1)}, bf16[1024]{0:T(1024)(128)(2,1)S...) all-reduce(bf16[1024]{0:T(1024)(128)(2,1)S(1)} %dynamic-update-slic, ...), channel_id=1, replica_groups=mesh['shard'=16,'replica'=2] {'shard'}, use_global_device_ids=true, to_apply=%add.3 | all-reduce | flops 8192 | bytes 32768
  83.4 17.3 %all-gather = bf16[16,1,256]{2,1,0:T(2,128)(2,1)S(1)} all-gather(bf16[1,1,256]{2,1,0:T(2,128)(2,1)S(1)} %reshape.182), channel_id=1, replica_groups=mesh['shard'=16,'replica'=2] {'shard'}, dimensions={0}, use_global_device_ids=true | all-gather | bytes 8704 | tf_op jit(solution)/shard_map/all_gather | solution.py:115
  101.3 3.8 fusion.1
  106.6 11.5 %all-gather.8.cloned.1.call-done = bf16[1024,1024]{1,0:T(8,128)(2,1)} async-done(((bf16[64,1024]{1,0:T(8,128)(2,1)}), bf16[1024,1024]{1,0:T(8,128)(2,1)}) %all-gather.8.cloned.1.call-update) | async-done | bytes 2097168 | tf_op jit(solution)/shard_map/all_gather | solution.py:84
  118.1 2.1 fusion.52
  120.4 73.5 %all-gather.10.cloned.1.call-done = bf16[1024,4096]{1,0:T(8,128)(2,1)} async-done(((bf16[64,4096]{1,0:T(8,128)(2,1)}), bf16[1024,4096]{1,0:T(8,128)(2,1)}) %all-gather.10.cloned.1.call-update) | async-done | bytes 8388624 | tf_op jit(solution)/shard_map/all_gather | solution.py:114
  193.9 6.1 convolution_add_fusion
  200.0 69.1 %all-gather.12.cloned.1.call-done = bf16[4096,1024]{1,0:T(8,128)(2,1)} async-done(((bf16[256,1024]{1,0:T(8,128)(2,1)}), bf16[4096,1024]{1,0:T(8,128)(2,1)}) %all-gather.12.cloned.1.call-update) | async-done | bytes 8388624 | tf_op jit(solution)/shard_map/all_gather | solution.py:116
  269.1 7.8 fusion.55
  277.0 3.0 multiply_reduce_fusion.1
  280.3 2.8 fusion.33
  283.4 2.4 convolution_convert_fusion.1
  286.0 1.3 fusion.56
  287.4 2.1 convolution_convert_fusion
  289.5 2.3 fusion.49
  292.3 6.8 fusion.29
  300.5 8.2 fusion.19
  308.7 1.5 copy-done.2
  310.2 9.3 fusion.36
  319.6 34.3 %reduce-scatter.7.cloned.1.call-done = f32[64,1024]{1,0:T(8,128)} async-done(((f32[1024,1024]{1,0:T(8,128)}), f32[64,1024]{1,0:T(8,128)}) %reduce-scatter.7.cloned.1.call-update) | async-done | bytes 262160 | tf_op jit(solution)/shard_map/reduce_scatter | solution.py:218
  353.9 138.2 %reduce-scatter.5.cloned.1.call-done = f32[64,3072]{1,0:T(8,128)} async-done(((f32[1024,3072]{1,0:T(8,128)}), f32[64,3072]{1,0:T(8,128)}) %reduce-scatter.5.cloned.1.call-update) | async-done | bytes 786448 | tf_op jit(solution)/shard_map/reduce_scatter | solution.py:215
  492.2 182.4 %reduce-scatter.9.cloned.1.call-done = f32[64,4096]{1,0:T(8,128)} async-done(((f32[1024,4096]{1,0:T(8,128)}), f32[64,4096]{1,0:T(8,128)}) %reduce-scatter.9.cloned.1.call-update) | async-done | bytes 1048592 | tf_op jit(solution)/shard_map/reduce_scatter | solution.py:152
  674.6 182.3 %reduce-scatter.11.cloned.1.call-done = f32[256,1024]{1,0:T(8,128)} async-done(((f32[4096,1024]{1,0:T(8,128)}), f32[256,1024]{1,0:T(8,128)}) %reduce-scatter.11.cloned.1.call-update) | async-done | bytes 1048592 | tf_op jit(solution)/shard_map/reduce_scatter | solution.py:154
  858.3 6.0 multiply_reduce_fusion.2
  864.3 59.7 %all-reduce.17 = (f32[1024]{0:T(1024)S(1)}, f32[1024]{0:T(1024)S(1)}, f32[1024]{0:T(1024)S(1)}, f32[1024]{0:T(1024)S(1)}, f32[1024]{0:T(1024)S(1)}, /*index=5*/f...) all-reduce(f32[1024]{0:T(1024)S(1)} %get-tuple-element.17, ...), channel_id=2, replica_groups=mesh['shard'=16,'replica'=2] {'shard'}, use_global_device_ids=true, to_apply=%region_12.13.clone | all-reduce | flops 12288 | bytes 98304
  924.7 5.7 all-reduce.18
  930.4 2.2 multiply_add_fusion.1
  932.6 5.7 fusion.13
  938.3 6.7 all-reduce.23.cloned.1.call-done
  945.0 2.2 copy.75
  947.3 1.7 copy.76
  (117 shorter events, 17.7 us)
Async XLA Ops:
  7.2 93.6 %copy-start.1 = (f32[128,1024]{1,0:T(8,128)S(1)}, f32[128,1024]{1,0:T(8,128)}, u32[]{:S(2)}) copy-start(f32[128,1024]{1,0:T(8,128)} %param.16) | copy-start | bytes 1572868
  7.2 93.9 %copy-start.17 = (s32[1,128]{1,0:T(1,128)S(1)}, s32[1,128]{1,0:T(1,128)}, u32[]{:S(2)}) copy-start(s32[1,128]{1,0:T(1,128)} %param.17) | copy-start | bytes 1540
  7.2 94.0 %all-gather.6.cloned.1.call-start = ((), (), s32[]{:S(2)}) async-start(), calls=%async_computation.4 | async-start | bytes 6684672 | tf_op jit(solution)/shard_map/all_gather | solution.py:81
  7.9 110.1 %all-gather.8.cloned.1.call-start = ((), (), s32[]{:S(2)}) async-start(), calls=%async_computation.5 | async-start | bytes 2228224 | tf_op jit(solution)/shard_map/all_gather | solution.py:84
  8.7 185.2 %all-gather.10.cloned.1.call-start = ((), (), s32[]{:S(2)}) async-start(), calls=%async_computation.6 | async-start | bytes 8912896 | tf_op jit(solution)/shard_map/all_gather | solution.py:114
  9.4 259.7 %all-gather.12.cloned.1.call-start = ((), (), s32[]{:S(2)}) async-start(), calls=%async_computation.7 | async-start | bytes 8912896 | tf_op jit(solution)/shard_map/all_gather | solution.py:116
  10.0 343.9 %reduce-scatter.7.cloned.1.call-start = ((), (), s32[]{:S(2)}) async-start(), calls=%async_computation.9 | async-start | bytes 4456448 | tf_op jit(solution)/shard_map/reduce_scatter | solution.py:218
  105.3 1.2 copy-start.6
  105.5 1.1 copy-start.11
  105.7 0.9 copy-start.9
  269.1 7.8 copy-start
  276.9 3.1 copy-start.4
  276.9 3.1 copy-start.8
  280.3 3.1 copy-start.3
  283.1 2.9 copy-start.7
  283.1 4.2 copy-start.12
  283.1 209.0 %reduce-scatter.5.cloned.1.call-start = ((), (), s32[]{:S(2)}) async-start(), calls=%async_computation.8 | async-start | bytes 13369344 | tf_op jit(solution)/shard_map/reduce_scatter | solution.py:215
  285.8 3.6 copy-start.10
  289.5 9.7 %copy-start.15 = (bf16[16,64,128]{2,1,0:T(8,128)(2,1)}, bf16[16,64,128]{2,1,0:T(8,128)(2,1)S(1)}, u32[]{:S(2)}) copy-start(bf16[16,64,128]{2,1,0:T(8,128)(2,1)S(1)} %convolution_convert_fusion) | copy-start | bytes 786436
  291.8 7.4 copy-start.16
  299.2 1.3 copy-start.5
  299.2 375.4 %reduce-scatter.9.cloned.1.call-start = ((), (), s32[]{:S(2)}) async-start(), calls=%async_computation.10 | async-start | bytes 17825792 | tf_op jit(solution)/shard_map/reduce_scatter | solution.py:152
  308.6 1.6 copy-start.2
  308.7 548.2 %reduce-scatter.11.cloned.1.call-start = ((), (), s32[]{:S(2)}) async-start(), calls=%async_computation.11 | async-start | bytes 17825792 | tf_op jit(solution)/shard_map/reduce_scatter | solution.py:154
  319.6 625.5 %all-reduce.23.cloned.1.call-start = ((), (), s32[]{:S(2)}) async-start(), calls=%async_computation.12 | async-start | bytes 6291456 | tf_op jit(solution)/shard_map/psum | solution.py:229
  945.0 3.9 copy-start.14
  945.0 4.9 copy-start.13
Sparse Core Ops, SparseCore 0:
  10.3 65.4 all-gather.5
  78.0 40.0 all-gather.7
  120.2 73.6 all-gather.9
  195.9 73.1 all-gather.11
  283.2 70.6 reduce-scatter.6
  358.4 133.7 reduce-scatter.4
  496.8 177.7 reduce-scatter.8
  679.3 177.5 reduce-scatter.10
  859.5 85.5 all-reduce.22
where the time goes:
time: 958 us; the launch traced here: 957 us
  waiting for transfers between devices  701 us (73%)
  blocking collectives  147 us (15%)
  matrix products  71 us (7%)
  local copies, waits for them, and re-layouts  18.9 us (2%)
  between operations  16.3 us (2%)
    reduce_scatter x1, waiting for transfers between devices, on_device(): lax.psum_scatter(grad_fc_weight, 'shard', scatter_dimension=0, tiled=True)  182 us
    reduce_scatter x1, waiting for transfers between devices, on_device(): lax.psum_scatter(grad_proj_weight, 'shard', scatter_dimension=0, tiled=True)  182 us
    reduce_scatter x1, waiting for transfers between devices, on_device(): lax.psum_scatter(grad_qkv_weight, 'shard', scatter_dimension=0, tiled=True)  138 us
    unnamed x2, blocking collectives  124 us
    all_gather x1, waiting for transfers between devices, on_device(): lax.all_gather(fc_weight, 'shard', axis=0, tiled=True)  73.5 us
    all_gather x1, waiting for transfers between devices, on_device(): lax.all_gather(proj_weight, 'shard', axis=0, tiled=True)  69.1 us
    dot_general x8, matrix products, contract(): lax.dot_general(left, right, (((left_axis,), (right_axis,)), ((), ())), p...  46.3 us
    reduce_scatter x1, waiting for transfers between devices, on_device(): lax.psum_scatter(grad_out_weight, 'shard', scatter_dimension=0, tiled=True)  34.3 us
  transfers between devices with their start and end apart: 9, of which 8 were waited for; matrix products, arithmetic and copies ran while one was open for 7% of the time, Pallas kernels for 0%

commit v1 on v0

v1 whole, which is shorter than its diff:
```python
import jax
import jax.numpy as jnp
from jax import lax
from jax.sharding import Mesh
from jax.sharding import PartitionSpec as P

HEADS = 16
HEAD = 64


EPS = 1e-05
GELU_C = 0.7978845608028654
GELU_A = 0.044715

GB = 4
GV = 2
B_AXES = ("bh", "bl")
G_AXES = ("bh", "bl", "v")
S_AXES = ("a", "bh", "bl")
ALL_AXES = ("a", "bh", "bl", "u", "v")
F32 = jnp.float32
BF16 = jnp.bfloat16


def layer_norm(values, gain, shift):
    row_mean = jnp.mean(values, axis=-1, keepdims=True)
    centered = values - row_mean
    inv_std = lax.rsqrt(jnp.mean(centered * centered, axis=-1, keepdims=True) + EPS)
    normed = centered * inv_std
    return (normed * gain + shift, normed, inv_std)


def norm_back(grad_out, normed, inv_std, gain):
    scaled = grad_out * gain
    return inv_std * (
        scaled
        - jnp.mean(scaled, axis=-1, keepdims=True)
        - normed * jnp.mean(scaled * normed, axis=-1, keepdims=True)
    )


def gelu_pair(pre_act):
    tangent = jnp.tanh(GELU_C * (pre_act + GELU_A * pre_act * pre_act * pre_act))
    value = 0.5 * pre_act * (1.0 + tangent)
    slope = 0.5 * (1.0 + tangent) + 0.5 * pre_act * (1.0 - tangent * tangent) * GELU_C * (
        1.0 + 3.0 * GELU_A * pre_act * pre_act
    )
    return (value, slope)


def contract(left, right, left_axis, right_axis):
    return lax.dot_general(
        left, right, (((left_axis,), (right_axis,)), ((), ())), preferred_element_type=F32
    )


def pick(values, index, axis):
    return lax.dynamic_index_in_dim(values, index, axis, keepdims=False)


def gather_group(values):
    return lax.all_gather(values, G_AXES, axis=0, tiled=True)


def scatter_group(values):
    return lax.psum_scatter(
        values.astype(BF16), G_AXES, scatter_dimension=0, tiled=True
    ).astype(F32)


def on_device(
    tokens,
    segment_ids,
    cotangent,
    norm1_gain,
    norm1_shift,
    qkv_weight,
    query_bias,
    value_bias,
    out_weight,
    out_bias,
    norm2_gain,
    norm2_shift,
    fc_weight,
    fc_bias,
    proj_weight,
    proj_bias,
):
    rows, width = tokens.shape
    n_a = lax.axis_size("a")
    n_bl = lax.axis_size("bl")
    n_bh = lax.axis_size("bh")
    n_u = lax.axis_size("u")
    shards = n_a * GB
    depth = width // shards
    hidden_rows = fc_bias.shape[0]
    hidden = hidden_rows * shards
    half = hidden_rows // GV
    my_hidden = n_a * half
    heads_here = HEADS // (GB * GV)
    cols = heads_here * HEAD
    scale = HEAD ** (-0.5)
    v = lax.axis_index("v")
    bl = lax.axis_index("bl")
    bh = lax.axis_index("bh")
    b = bh * n_bl + bl
    me = lax.axis_index("a") * GB + b

    small = jnp.concatenate(
        [
            norm1_gain,
            norm1_shift,
            query_bias,
            value_bias,
            out_bias,
            norm2_gain,
            norm2_shift,
            proj_bias,
            fc_bias,
        ]
    )
    small = lax.all_gather(small, S_AXES, axis=0).astype(F32)
    gain1, shift1, bias_query, bias_value, bias_out, gain2, shift2, bias_proj = (
        small[:, i * depth : (i + 1) * depth].reshape(width) for i in range(8)
    )
    bias_fc = small[:, 8 * depth :]

    def head_split(values):
        lead = values.shape[:-1]
        n = len(lead)
        values = values.reshape(*lead, n_bl, GV, heads_here, n_bh, HEAD)
        order = (n + 3, n, n + 1, *range(n), n + 2, n + 4)
        return values.transpose(order).reshape(n_bh, n_bl, GV, *lead, cols)

    qkv = pick(head_split(qkv_weight.reshape(depth, 3, width)), v, 2)
    qkv = qkv.reshape(GB, depth, 3 * cols)
    fc = pick(fc_weight.reshape(depth, n_a, GB, GV, half), v, 3)
    fc = fc.transpose(2, 0, 1, 3).reshape(GB, depth, my_hidden)
    qkv = lax.all_to_all(qkv, B_AXES, 0, 0, tiled=True).reshape(GB * depth, 3 * cols)
    fc = lax.all_to_all(fc, B_AXES, 0, 0, tiled=True).reshape(GB * depth, my_hidden)
    w_qkv = lax.all_gather(qkv, "a", axis=0, tiled=True)
    w_out = lax.all_gather(out_weight, ("a", "bl"), axis=0, tiled=True)
    slot = bl * GV + v
    w_out = lax.dynamic_slice_in_dim(w_out, slot * cols, cols, 0)
    w_fc = lax.all_gather(fc, "a", axis=0, tiled=True)
    w_proj = lax.all_gather(
        lax.dynamic_slice_in_dim(proj_weight, v * half, half, 0), "a", axis=0, tiled=True
    )

    def my_heads(values):
        return pick(head_split(values).reshape(GB, GV, cols), b, 0)

    bq = pick(my_heads(bias_query), v, 0)
    bv = pick(my_heads(bias_value), v, 0)
    b_fc = pick(pick(bias_fc.reshape(n_a, GB, GV, half), b, 1), v, 1).reshape(my_hidden)

    cot_low = gather_group(cotangent.astype(BF16))
    segments = lax.all_gather(segment_ids[0], G_AXES, axis=0)

    ln1, normed1, inv1 = layer_norm(tokens, gain1, shift1)
    input1 = gather_group(ln1.astype(BF16))
    blocks = GB * GV
    qkv_bias = jnp.concatenate([bq, jnp.zeros((cols,), F32), bv])
    projected = jnp.dot(input1, w_qkv, preferred_element_type=F32) + qkv_bias
    projected = projected.astype(BF16).reshape(blocks, rows, 3, heads_here, HEAD)
    query, keyed, valued = projected[:, :, 0], projected[:, :, 1], projected[:, :, 2]
    scores = jnp.einsum("nqhd,nkhd->nhqk", query, keyed, preferred_element_type=F32) * scale
    position = jnp.arange(rows)
    allowed = (segments[:, :, None] == segments[:, None, :]) & (
        position[None, :] <= position[:, None]
    )
    scores = jnp.where(allowed[:, None], scores, -1e30)
    top = jnp.max(scores, axis=-1, keepdims=True)
    log_total = top + jnp.log(jnp.sum(jnp.exp(scores - top), axis=-1, keepdims=True))
    probs = jnp.exp(scores - log_total)
    probs_low = probs.astype(BF16)
    context = jnp.einsum("nhqk,nkhd->nqhd", probs_low, valued, preferred_element_type=F32)
    context = context.reshape(blocks * rows, cols).astype(BF16)
    middle = (
        tokens + scatter_group(jnp.dot(context, w_out, preferred_element_type=F32)) + bias_out
    )

    ln2, normed2, inv2 = layer_norm(middle, gain2, shift2)
    input2 = gather_group(ln2.astype(BF16))
    pre_act = jnp.dot(input2, w_fc, preferred_element_type=F32) + b_fc
    gelu_value, gelu_slope = gelu_pair(pre_act)
    activated = gelu_value.astype(BF16)
    grad_pre = contract(cot_low, w_proj, 1, 1) * gelu_slope
    grad_pre_low = grad_pre.astype(BF16)
    grad_in2 = scatter_group(contract(grad_pre_low, w_fc, 1, 1))
    output = (
        middle + scatter_group(jnp.dot(activated, w_proj, preferred_element_type=F32)) + bias_proj
    )
    grad_fc_bias = jnp.sum(grad_pre, axis=0)
    grad_proj_weight = contract(activated, cot_low, 0, 0)
    grad_fc_weight = contract(input2, grad_pre_low, 0, 0)

    def reduce_a(values, axes="a"):
        values = lax.psum_scatter(values.astype(BF16), axes, scatter_dimension=0, tiled=True)
        return lax.psum(values, "u") if n_u > 1 else values

    share_proj = lax.all_gather(reduce_a(grad_proj_weight), "v", axis=0, tiled=True).astype(F32)

    def columns_home(values):
        values = reduce_a(values).reshape(GB, depth, values.shape[1])
        values = lax.all_to_all(values, B_AXES, 0, 0, tiled=True)
        return lax.all_gather(values, "v", axis=0)

    share_fc = columns_home(grad_fc_weight).reshape(GV, GB, depth, n_a, half)
    share_fc = share_fc.transpose(2, 3, 1, 0, 4).reshape(depth, hidden).astype(F32)

    grad_gain2 = jnp.sum(grad_in2 * normed2, axis=0)
    grad_shift2 = jnp.sum(grad_in2, axis=0)
    grad_middle = cotangent + norm_back(grad_in2, normed2, inv2, gain2)

    mid_low = gather_group(grad_middle.astype(BF16))
    grad_out_weight = contract(context, mid_low, 0, 0)
    grad_context = contract(mid_low, w_out, 1, 1)
    grad_context = grad_context.astype(BF16).reshape(blocks, rows, heads_here, HEAD)
    grad_value = jnp.einsum("nhqk,nqhd->nkhd", probs_low, grad_context, preferred_element_type=F32)
    grad_probs = jnp.einsum("nqhd,nkhd->nhqk", grad_context, valued, preferred_element_type=F32)
    grad_scores = probs * (grad_probs - jnp.sum(probs * grad_probs, axis=-1, keepdims=True)) * scale
    grad_scores = grad_scores.astype(BF16)
    grad_query = jnp.einsum("nhqk,nkhd->nqhd", grad_scores, keyed, preferred_element_type=F32)
    grad_key = jnp.einsum("nhqk,nqhd->nkhd", grad_scores, query, preferred_element_type=F32)
    grad_query, grad_key, grad_value = (
        g.reshape(blocks * rows, cols) for g in (grad_query, grad_key, grad_value)
    )
    grad_query_bias = jnp.sum(grad_query, axis=0)
    grad_value_bias = jnp.sum(grad_value, axis=0)
    grad_qkv = jnp.concatenate([grad_query, grad_key, grad_value], axis=1).astype(BF16)
    grad_in1 = scatter_group(contract(grad_qkv, w_qkv, 1, 1))
    grad_qkv_weight = contract(input1, grad_qkv, 0, 0)

    share_qkv = columns_home(grad_qkv_weight).reshape(
        GV, n_bh, n_bl, depth, 3, heads_here, HEAD
    )
    share_qkv = share_qkv.transpose(3, 4, 2, 0, 5, 1, 6).reshape(depth, 3 * width).astype(F32)

    out_full = jnp.zeros((depth * n_a * n_bl, width), BF16)
    out_full = lax.dynamic_update_slice_in_dim(
        out_full, grad_out_weight.astype(BF16), slot * cols, 0
    )
    share_out = lax.psum(reduce_a(out_full, ("a", "bl")), "v").astype(F32)

    grad_gain1 = jnp.sum(grad_in1 * normed1, axis=0)
    grad_shift1 = jnp.sum(grad_in1, axis=0)
    tokens_grad = grad_middle + norm_back(grad_in1, normed1, inv1, gain1)

    def heads_full(values):
        here = (jnp.arange(GB * GV) == b * GV + v).astype(F32)
        values = here[:, None] * values[None, :]
        values = values.reshape(n_bh, n_bl, GV, heads_here, HEAD).transpose(1, 2, 3, 0, 4)
        return values.reshape(width)

    here = (jnp.arange(GB * GV) == b * GV + v).astype(F32)
    fc_full = here.reshape(1, GB, GV, 1) * grad_fc_bias.reshape(n_a, 1, 1, half)
    sums = [
        jnp.sum(cotangent, axis=0),
        grad_gain2,
        grad_shift2,
        jnp.sum(grad_middle, axis=0),
        heads_full(grad_query_bias),
        heads_full(grad_value_bias),
        grad_gain1,
        grad_shift1,
    ]
    sums = [s.reshape(shards, depth) for s in sums]
    sums = jnp.concatenate([*sums, fc_full.reshape(shards, hidden_rows)], axis=1)
    sums = pick(lax.psum(sums, ALL_AXES), me, 0)
    (
        share_proj_bias,
        share_gain2,
        share_shift2,
        share_out_bias,
        share_query_bias,
        share_value_bias,
        share_gain1,
        share_shift1,
    ) = (sums[i * depth : (i + 1) * depth] for i in range(8))
    share_fc_bias = sums[8 * depth :]
    return (
        output,
        tokens_grad,
        share_gain1,
        share_shift1,
        share_qkv,
        share_query_bias,
        share_value_bias,
        share_out,
        share_out_bias,
        share_gain2,
        share_shift2,
        share_fc,
        share_fc_bias,
        share_proj,
        share_proj_bias,
    )


def solution(mesh):
    shard, replica = mesh.shape["shard"], mesh.shape["replica"]
    head_parts = max(1, HEAD * shard // (HEADS * HEAD))
    grid = mesh.devices.reshape(
        shard // GB, GB // head_parts, head_parts, replica // GV, GV
    )
    inner = Mesh(grid, ALL_AXES)
    row = P(ALL_AXES, None)
    vec = P(S_AXES)
    mat = P(S_AXES, None)
    in_specs = (
        row, row, row, vec, vec, mat, vec, vec, mat, vec, vec, vec, mat, vec, mat, vec,
    )
    out_specs = (
        row, row, vec, vec, mat, vec, vec, mat, vec, vec, vec, mat, vec, mat, vec,
    )
    return jax.shard_map(
        on_device, mesh=inner, in_specs=in_specs, out_specs=out_specs, check_vma=False
    )
```

time: 958 us -> 568 us (0.59)
  waiting for transfers between devices: 701 us -> 285 us
  local copies, waits for them, and re-layouts: 18.9 us -> 43.5 us
  matrix products: 71 us -> 50.8 us
  other arithmetic: 3.33 us -> 17.9 us
  starting transfers between devices: 0.58 us -> 11.2 us
    reduce_scatter x4 -> x8, waiting for transfers between devices: 537 us -> 172 us  [the longest x4 130 us: scatter_group(): lax.psum_scatter(values.astype(BF16), G_AXES, scatter_dimension=0, tiled=...]
    unnamed x2 -> x0, blocking collectives: 124 us -> none
    all_gather x1 -> x7, blocking collectives: 17.3 us -> 93.2 us  [the longest x1 23.2 us: on_device(): small = lax.all_gather(small, S_AXES, axis=0).astype(F32)]
    all_gather x4 -> x6, waiting for transfers between devices: 154 us -> 109 us  [the longest x4 83.4 us: gather_group(): return lax.all_gather(values, G_AXES, axis=0, tiled=True)]
    psum x1, blocking collectives: 5.7 us -> 39.7 us  [on_device(): sums = pick(lax.psum(sums, ALL_AXES), me, 0)]
    dot_general x8, matrix products: 46.3 us -> 27.7 us  [contract(): lax.dot_general(left, right, (((left_axis,), (right_axis,)), ((), ())), p...]
    convert_element_type x1 -> x8, local copies, waits for them, and re-layouts: 0.17 us -> 12.1 us  [the longest x3 6.63 us: on_device(): share_qkv.transpose(3, 4, 2, 0, 5, 1, 6).reshape(depth, 3 * width)]
    unnamed x67 -> x57, local copies, waits for them, and re-layouts: 18 us -> 7.82 us
  transfers between devices with their start and end apart: 9 -> 18, of which waited for: 8 -> 12; matrix products, arithmetic and copies ran while one was open for 7% -> 12% of each run, Pallas kernels for 0% -> 0%
where the time goes in v1:
time: 568 us; the launch traced here: 566 us
  waiting for transfers between devices  285 us (50%)
  blocking collectives  142 us (25%)
  matrix products  50.8 us (9%)
  local copies, waits for them, and re-layouts  43.5 us (8%)
  other arithmetic  17.9 us (3%)
  between operations  16 us (3%)
  starting transfers between devices  11.2 us (2%)
    reduce_scatter x4, waiting for transfers between devices, scatter_group(): lax.psum_scatter(values.astype(BF16), G_AXES, scatter_dimension=0, tiled=...  130 us
    all_gather x4, waiting for transfers between devices, gather_group(): return lax.all_gather(values, G_AXES, axis=0, tiled=True)  83.4 us
    reduce_scatter x4, waiting for transfers between devices, reduce_a(): lax.psum_scatter(values.astype(BF16), axes, scatter_dimension=0, tiled=True)  41.8 us
    psum x1, blocking collectives, on_device(): sums = pick(lax.psum(sums, ALL_AXES), me, 0)  39.7 us
    dot_general x8, matrix products, contract(): lax.dot_general(left, right, (((left_axis,), (right_axis,)), ((), ())), p...  27.7 us
    all_gather x1, waiting for transfers between devices, on_device(): lax.all_gather(lax.dynamic_slice_in_dim(proj_weight, v * half, half, 0),...  25.6 us
    all_gather x1, blocking collectives, on_device(): small = lax.all_gather(small, S_AXES, axis=0).astype(F32)  23.2 us
    all_gather x1, blocking collectives, on_device(): w_qkv = lax.all_gather(qkv, 'a', axis=0, tiled=True)  17.1 us
  transfers between devices with their start and end apart: 18, of which 12 were waited for; matrix products, arithmetic and copies ran while one was open for 12% of the time, Pallas kernels for 0%

profile of v1, /device:TPU:0, one launch (start us, length us, event | category | flops | bytes accessed | tf_op | source)
XLA Modules:
  0.0 566.3 jit_solution(9281772246037564233)
XLA Ops:
  8.1 6.2 %concatenate.13 = bf16[768]{0:T(1024)(128)(2,1)S(1)} concatenate(bf16[64]{0:T(256)(128)(2,1)} %param.19, bf16[64]{0:T(256)(128)(2,1)} %param.20, bf16[64]{0:T(256)(128)(2,1)} %param.22, bf16[64]{0:T(256)(128)(2,1)} %param.23, bf16[64]{0:T(256)(128)(2,1)} %param.25, bf16[64]{0:T(256)(128)(2,1)} %param.26, bf16[64]{0:T(256)(128)(2,1)} %param.27, bf16[64]{0:T(256)(128)(2,1)} %param.31, ...), dimensions={0} | concatenate | bytes 3072 | tf_op jit(solution)/shard_map/concatenate | solution.py:109
  14.3 23.2 %all-gather.3 = bf16[16,1,768]{2,1,0:T(2,128)(2,1)S(1)} all-gather(bf16[1,1,768]{2,1,0:T(2,128)(2,1)S(1)} %reshape.289), channel_id=2, replica_groups=mesh['a'=4,'bh'=4,'bl'=1,'u'=1,'v'=2] {'a','bh','bl'}, dimensions={0}, use_global_device_ids=true | all-gather | bytes 26112 | tf_op jit(solution)/shard_map/all_gather | solution.py:122
  45.4 3.4 all-to-all-start
  49.0 12.5 %all-gather.4 = s32[8,1,128]{2,1,0:T(1,128)S(1)} all-gather(s32[1,1,128]{2,1,0:T(1,128)S(1)} %bitcast.183), channel_id=1, replica_groups=mesh['a'=4,'bh'=4,'bl'=1,'u'=1,'v'=2] {'bh','bl','v'}, dimensions={0}, use_global_device_ids=true | all-gather | bytes 4608 | tf_op jit(solution)/shard_map/all_gather | solution.py:158
  61.6 17.0 %all_gather.53 = bf16[256,1024]{1,0:T(8,128)(2,1)} all-gather(bf16[64,1024]{1,0:T(8,128)(2,1)S(1)} %copy-done.14), channel_id=1, replica_groups=mesh['a'=4,'bh'=4,'bl'=1,'u'=1,'v'=2] {'a','bl'}, dimensions={0}, use_global_device_ids=true | all-gather | bytes 655360 | tf_op jit(solution)/shard_map/all_gather | solution.py:142
  78.9 17.1 %all_gather.51 = bf16[1024,384]{1,0:T(8,128)(2,1)S(1)} all-gather(bf16[256,384]{1,0:T(8,128)(2,1)S(1)} %bitcast.162), channel_id=1, replica_groups=mesh['a'=4,'bh'=4,'bl'=1,'u'=1,'v'=2] {'a'}, dimensions={0}, use_global_device_ids=true | all-gather | bytes 983040 | tf_op jit(solution)/shard_map/all_gather | solution.py:141
  112.5 9.1 %all_to_all.20 = bf16[4,64,512]{2,1,0:T(8,128)(2,1)} all-to-all(bf16[4,64,512]{2,1,0:T(8,128)(2,1)S(1)} %copy_bitcast_fusion.1), channel_id=1, replica_groups=mesh['a'=4,'bh'=4,'bl'=1,'u'=1,'v'=2] {'bh','bl'}, dimensions={0} | all-to-all | bytes 524288 | tf_op jit(solution)/shard_map/all_to_all | solution.py:140
  121.9 28.5 %reduce-scatter.9.cloned.1.call-done = bf16[128,1024]{1,0:T(8,128)(2,1)} async-done(((bf16[1024,1024]{1,0:T(8,128)(2,1)}), bf16[128,1024]{1,0:T(8,128)(2,1)}) %reduce-scatter.9.cloned.1.call-update) | async-done | bytes 262160 | tf_op jit(solution)/shard_map/reduce_scatter | solution.py:66
  154.6 25.9 %all-gather.14.cloned.1.call-done = bf16[1024,1024]{1,0:T(8,128)(2,1)} async-done(((bf16[128,1024]{1,0:T(8,128)(2,1)}), bf16[1024,1024]{1,0:T(8,128)(2,1)}) %all-gather.14.cloned.1.call-update) | async-done | bytes 2097168 | tf_op jit(solution)/shard_map/all_gather | solution.py:62
  180.4 4.4 fusion.81
  184.9 25.6 %all-gather.18.cloned.1.call-done = bf16[512,1024]{1,0:T(8,128)(2,1)} async-done(((bf16[128,1024]{1,0:T(8,128)(2,1)}), bf16[512,1024]{1,0:T(8,128)(2,1)}) %all-gather.18.cloned.1.call-update) | async-done | bytes 1048592 | tf_op jit(solution)/shard_map/all_gather | solution.py:146
  210.4 29.8 %all-gather.20.cloned.1.call-done = bf16[1024,1024]{1,0:T(8,128)(2,1)} async-done(((bf16[128,1024]{1,0:T(8,128)(2,1)}), bf16[1024,1024]{1,0:T(8,128)(2,1)}) %all-gather.20.cloned.1.call-update) | async-done | bytes 2097168 | tf_op jit(solution)/shard_map/all_gather | solution.py:62
  240.2 5.0 fusion.80
  249.0 4.7 convolution_convert_fusion.2
  253.8 36.5 %reduce-scatter.13.cloned.1.call-done = bf16[128,1024]{1,0:T(8,128)(2,1)} async-done(((bf16[1024,1024]{1,0:T(8,128)(2,1)}), bf16[128,1024]{1,0:T(8,128)(2,1)}) %reduce-scatter.13.cloned.1.call-update) | async-done | bytes 262160 | tf_op jit(solution)/shard_map/reduce_scatter | solution.py:66
  291.6 43.1 %reduce-scatter.11.cloned.1.call-done = bf16[128,1024]{1,0:T(8,128)(2,1)} async-done(((bf16[1024,1024]{1,0:T(8,128)(2,1)}), bf16[128,1024]{1,0:T(8,128)(2,1)}) %reduce-scatter.11.cloned.1.call-update) | async-done | bytes 262160 | tf_op jit(solution)/shard_map/reduce_scatter | solution.py:66
  337.7 27.8 %all-gather.22.cloned.1.call-done = bf16[1024,1024]{1,0:T(8,128)(2,1)} async-done(((bf16[128,1024]{1,0:T(8,128)(2,1)}), bf16[1024,1024]{1,0:T(8,128)(2,1)}) %all-gather.22.cloned.1.call-update) | async-done | bytes 2097168 | tf_op jit(solution)/shard_map/all_gather | solution.py:62
  368.6 4.1 convolution_convert_fusion.5
  372.8 4.7 convolution_convert_fusion.4
  377.8 3.0 convolution_convert_fusion.9
  398.7 3.8 convolution_convert_fusion
  402.7 15.9 %reduce-scatter.21.cloned.1.call-done = bf16[256,512]{1,0:T(8,128)(2,1)} async-done(((bf16[1024,512]{1,0:T(8,128)(2,1)}), bf16[256,512]{1,0:T(8,128)(2,1)}) %reduce-scatter.21.cloned.1.call-update) | async-done | bytes 262160 | tf_op jit(solution)/shard_map/reduce_scatter | solution.py:199
  418.7 3.4 all-to-all-start.3
  422.2 24.4 %reduce-scatter.23.cloned.1.call-done = bf16[128,1024]{1,0:T(8,128)(2,1)} async-done(((bf16[512,1024]{1,0:T(8,128)(2,1)}), bf16[128,1024]{1,0:T(8,128)(2,1)}) %reduce-scatter.23.cloned.1.call-update) | async-done | bytes 262160 | tf_op jit(solution)/shard_map/reduce_scatter | solution.py:199
  446.5 8.6 %all_gather.63 = bf16[256,1024]{1,0:T(8,128)(2,1)S(1)} all-gather(bf16[128,1024]{1,0:T(8,128)(2,1)} %reduce-scatter.23.cloned.1.call-done), channel_id=1, replica_groups=mesh['a'=4,'bh'=4,'bl'=1,'u'=1,'v'=2] {'v'}, dimensions={0}, use_global_device_ids=true | all-gather | bytes 786432 | tf_op jit(solution)/shard_map/all_gather | solution.py:202
  456.2 7.4 %all-gather.2 = bf16[8,64,512]{2,1,0:T(8,128)(2,1)S(1)} all-gather(bf16[4,64,512]{2,1,0:T(8,128)(2,1)S(1)} %all-to-all-done.3), channel_id=4, replica_groups=mesh['a'=4,'bh'=4,'bl'=1,'u'=1,'v'=2] {'v'}, dimensions={0}, use_global_device_ids=true | all-gather | bytes 786432 | tf_op jit(solution)/shard_map/all_gather | solution.py:207
  465.8 3.0 reshape.278
  470.4 3.4 all-to-all-start.2
  475.5 3.6 all-to-all-done.2
  479.1 7.4 %all-gather.1 = bf16[8,64,384]{2,1,0:T(8,128)(2,1)S(1)} all-gather(bf16[4,64,384]{2,1,0:T(8,128)(2,1)S(1)} %all-to-all-done.2), channel_id=3, replica_groups=mesh['a'=4,'bh'=4,'bl'=1,'u'=1,'v'=2] {'v'}, dimensions={0}, use_global_device_ids=true | all-gather | bytes 589824 | tf_op jit(solution)/shard_map/all_gather | solution.py:207
  493.1 21.6 %reduce-scatter.15.cloned.1.call-done = bf16[128,1024]{1,0:T(8,128)(2,1)} async-done(((bf16[1024,1024]{1,0:T(8,128)(2,1)}), bf16[128,1024]{1,0:T(8,128)(2,1)}) %reduce-scatter.15.cloned.1.call-update) | async-done | bytes 262160 | tf_op jit(solution)/shard_map/reduce_scatter | solution.py:66
  516.2 39.7 %psum.14 = f32[16,768]{1,0:T(8,128)S(1)} all-reduce(f32[16,768]{1,0:T(8,128)S(1)} %concatenate.16), channel_id=1, replica_groups=mesh['a'=4,'bh'=4,'bl'=1,'u'=1,'v'=2] {'a','bh','bl','u','v'}, use_global_device_ids=true, to_apply=%region_24.25 | all-reduce | flops 12288 | bytes 98304 | tf_op jit(solution)/shard_map/psum | solution.py:270
  (188 shorter events, 76.5 us)
Async XLA Ops:
  8.0 144.6 %copy-start = (bf16[256,1024]{1,0:T(8,128)(2,1)S(1)}, bf16[256,1024]{1,0:T(8,128)(2,1)}, u32[]{:S(2)}) copy-start(bf16[256,1024]{1,0:T(8,128)(2,1)} %param.30) | copy-start | bytes 1572868
  8.0 34.6 %copy-start.12 = (bf16[64,3072]{1,0:T(8,128)(2,1)S(1)}, bf16[64,3072]{1,0:T(8,128)(2,1)}, u32[]{:S(2)}) copy-start(bf16[64,3072]{1,0:T(8,128)(2,1)} %param.21) | copy-start | bytes 1179652
  8.0 87.9 %all-gather.12.cloned.1.call-start = ((), (), s32[]{:S(2)}) async-start(), calls=%async_computation.12 | async-start | bytes 2359296 | tf_op jit(solution)/shard_map/all_gather | solution.py:62
  37.5 6.5 %copy-start.13 = (f32[16,768]{1,0:T(8,128)}, f32[16,768]{1,0:T(8,128)S(1)}, u32[]{:S(2)}) copy-start(f32[16,768]{1,0:T(8,128)S(1)} %bitcast_convert_fusion) | copy-start | bytes 147460
  43.1 5.9 %copy-start.21 = (s32[1,128]{1,0:T(1,128)S(1)}, s32[1,128]{1,0:T(1,128)}, u32[]{:S(2)}) copy-start(s32[1,128]{1,0:T(1,128)} %param.17) | copy-start | bytes 1540
  43.2 18.4 %copy-start.14 = (bf16[64,1024]{1,0:T(8,128)(2,1)S(1)}, bf16[64,1024]{1,0:T(8,128)(2,1)}, u32[]{:S(2)}) copy-start(bf16[64,1024]{1,0:T(8,128)(2,1)} %param.24) | copy-start | bytes 393220
  45.4 33.5 %all-to-all-start = ((bf16[4,64,384]{2,1,0:T(8,128)(2,1)}), bf16[4,64,384]{2,1,0:T(8,128)(2,1)S(1)}, u32[]{:S(2)}, u32[]{:S(2)}) async-start(bf16[4,64,384]{2,1,0:T(8,128)(2,1)} %reshape.258), calls=%async_computation | async-start | bytes 393216 | tf_op jit(solution)/shard_map/all_to_all | solution.py:139
  48.8 101.6 %reduce-scatter.9.cloned.1.call-start = ((), (), s32[]{:S(2)}) async-start(), calls=%async_computation.13 | async-start | bytes 2359296 | tf_op jit(solution)/shard_map/reduce_scatter | solution.py:66
  110.4 11.3 %copy-start.18 = (f32[16,64]{1,0:T(8,128)S(1)}, f32[16,64]{1,0:T(8,128)}, u32[]{:S(2)}) copy-start(f32[16,64]{1,0:T(8,128)} %get-tuple-element.48) | copy-start | bytes 12292
  110.4 11.3 %copy-start.17 = (f32[16,64]{1,0:T(8,128)S(1)}, f32[16,64]{1,0:T(8,128)}, u32[]{:S(2)}) copy-start(f32[16,64]{1,0:T(8,128)} %get-tuple-element.47) | copy-start | bytes 12292
  110.4 11.4 %copy-start.16 = (f32[16,64]{1,0:T(8,128)S(1)}, f32[16,64]{1,0:T(8,128)}, u32[]{:S(2)}) copy-start(f32[16,64]{1,0:T(8,128)} %get-tuple-element.46) | copy-start | bytes 12292
  110.4 40.0 %copy-start.1 = (f32[128,1024]{1,0:T(8,128)S(1)}, f32[128,1024]{1,0:T(8,128)}, u32[]{:S(2)}) copy-start(f32[128,1024]{1,0:T(8,128)} %param.16) | copy-start | bytes 1572868
  110.4 44.1 %all-gather.16.cloned.1.call-start = ((), (), s32[]{:S(2)}) async-start(), calls=%async_computation.15 | async-start | bytes 1310720 | tf_op jit(solution)/shard_map/all_gather | solution.py:145
  121.6 31.9 %copy-start.4 = (f32[128,1024]{1,0:T(8,128)S(1)}, f32[128,1024]{1,0:T(8,128)}, u32[]{:S(2)}) copy-start(f32[128,1024]{1,0:T(8,128)} %param.18) | copy-start | bytes 1572868
  121.6 58.8 %all-gather.14.cloned.1.call-start = ((), (), s32[]{:S(2)}) async-start(), calls=%async_computation.14 | async-start | bytes 2359296 | tf_op jit(solution)/shard_map/all_gather | solution.py:62
  121.9 32.6 %slice-start = ((f32[16,768]{1,0:T(8,128)}), f32[16,256]{1,0:T(8,128)S(1)}, s32[]{:S(2)}) async-start(f32[16,768]{1,0:T(8,128)} %copy-done.13), calls=%async_computation.27 | async-start | bytes 32768 | tf_op jit(solution)/shard_map/slice | solution.py:126
  152.6 57.8 %all-gather.18.cloned.1.call-start = ((), (), s32[]{:S(2)}) async-start(), calls=%async_computation.16 | async-start | bytes 1310720 | tf_op jit(solution)/shard_map/all_gather | solution.py:146
  153.4 86.8 %all-gather.20.cloned.1.call-start = ((), (), s32[]{:S(2)}) async-start(), calls=%async_computation.18 | async-start | bytes 2359296 | tf_op jit(solution)/shard_map/all_gather | solution.py:62
  154.2 136.1 %reduce-scatter.13.cloned.1.call-start = ((), (), s32[]{:S(2)}) async-start(), calls=%async_computation.19 | async-start | bytes 2359296 | tf_op jit(solution)/shard_map/reduce_scatter | solution.py:66
  240.2 6.0 %copy-start.23 = (bf16[1024,512]{1,0:T(8,128)(2,1)S(1)}, bf16[1024,512]{1,0:T(8,128)(2,1)}, u32[]{:S(2)}) copy-start(bf16[1024,512]{1,0:T(8,128)(2,1)} %all-gather.16.cloned.1.call-done) | copy-start | bytes 3145732
  248.9 85.8 %reduce-scatter.11.cloned.1.call-start = ((), (), s32[]{:S(2)}) async-start(), calls=%async_computation.17 | async-start | bytes 2359296 | tf_op jit(solution)/shard_map/reduce_scatter | solution.py:66
  253.7 111.8 %all-gather.22.cloned.1.call-start = ((), (), s32[]{:S(2)}) async-start(), calls=%async_computation.20 | async-start | bytes 2359296 | tf_op jit(solution)/shard_map/all_gather | solution.py:62
  337.7 60.5 %reduce-scatter.19.cloned.1.call-start = ((), (), s32[]{:S(2)}) async-start(), calls=%async_computation.23 | async-start | bytes 655360 | tf_op jit(solution)/shard_map/reduce_scatter | solution.py:199
  368.6 50.1 %reduce-scatter.21.cloned.1.call-start = ((), (), s32[]{:S(2)}) async-start(), calls=%async_computation.25 | async-start | bytes 1310720 | tf_op jit(solution)/shard_map/reduce_scatter | solution.py:199
  372.8 73.8 %reduce-scatter.23.cloned.1.call-start = ((), (), s32[]{:S(2)}) async-start(), calls=%async_computation.26 | async-start | bytes 1310720 | tf_op jit(solution)/shard_map/reduce_scatter | solution.py:199
  377.6 92.9 %reduce-scatter.17.cloned.1.call-start = ((), (), s32[]{:S(2)}) async-start(), calls=%async_computation.22 | async-start | bytes 983040 | tf_op jit(solution)/shard_map/reduce_scatter | solution.py:199
  385.6 5.3 copy-start.7
  398.1 75.8 %all-reduce.2.cloned.1.call-start = ((), (), s32[]{:S(2)}) async-start(), calls=%async_computation.24 | async-start | bytes 262144 | tf_op jit(solution)/shard_map/psum | solution.py:244
  398.7 116.0 %reduce-scatter.15.cloned.1.call-start = ((), (), s32[]{:S(2)}) async-start(), calls=%async_computation.21 | async-start | bytes 2359296 | tf_op jit(solution)/shard_map/reduce_scatter | solution.py:66
  418.7 37.5 %all-to-all-start.3 = ((bf16[4,64,512]{2,1,0:T(8,128)(2,1)}), bf16[4,64,512]{2,1,0:T(8,128)(2,1)S(1)}, u32[]{:S(2)}, u32[]{:S(2)}) async-start(bf16[4,64,512]{2,1,0:T(8,128)(2,1)} %bitcast.163), calls=%async_computation.10 | async-start | bytes 524288 | tf_op jit(solution)/shard_map/all_to_all | solution.py:206
  470.4 8.7 %all-to-all-start.2 = ((bf16[4,64,384]{2,1,0:T(8,128)(2,1)}), bf16[4,64,384]{2,1,0:T(8,128)(2,1)S(1)}, u32[]{:S(2)}, u32[]{:S(2)}) async-start(bf16[4,64,384]{2,1,0:T(8,128)(2,1)} %bitcast.164), calls=%async_computation.7 | async-start | bytes 393216 | tf_op jit(solution)/shard_map/all_to_all | solution.py:206
  488.7 26.0 %copy-start.20 = (f32[128]{0:T(128)S(1)}, f32[128]{0:T(128)}, u32[]{:S(2)}) copy-start(f32[128]{0:T(128)} %copy-done.19) | copy-start | bytes 1540
  (12 other events, 27.9 us)
Sparse Core Ops, SparseCore 0:
  42.7 25.1 all-gather.11
  110.5 39.8 reduce-scatter.8
  249.0 41.2 reduce-scatter.12
  293.5 41.1 reduce-scatter.10
  400.9 21.4 all-reduce.1
Sparse Core Ops, SparseCore 1:
  121.7 25.9 all-gather.15
  152.7 27.7 all-gather.13
  182.5 27.8 all-gather.17
  213.1 27.1 all-gather.19
  337.8 27.7 all-gather.21
  368.7 21.5 reduce-scatter.18
  393.1 25.5 reduce-scatter.20
  420.8 25.7 reduce-scatter.22
  448.8 21.6 reduce-scatter.16
  474.1 40.6 reduce-scatter.14

commit v2 on v1

--- a/solution.py
+++ b/solution.py
@@ -1,6 +1,10 @@
+import functools
+
 import jax
 import jax.numpy as jnp
 from jax import lax
+from jax.experimental import pallas as pl
+from jax.experimental.pallas import tpu as pltpu
 from jax.sharding import Mesh
 from jax.sharding import PartitionSpec as P
 
@@ -14,10 +18,13 @@
 
 GB = 4
 GV = 2
-B_AXES = ("bh", "bl")
-G_AXES = ("bh", "bl", "v")
-S_AXES = ("a", "bh", "bl")
-ALL_AXES = ("a", "bh", "bl", "u", "v")
+G = GB * GV
+B_AXES = ("b1", "b0")
+G_AXES = ("b1", "b0", "v")
+S_AXES = ("a", "b1", "b0")
+ALL_AXES = ("a", "b1", "b0", "u", "v")
+MESH = pl.DeviceIdType.MESH
+VMEM = pl.BlockSpec(memory_space=pltpu.VMEM)
 F32 = jnp.float32
 BF16 = jnp.bfloat16
 
@@ -66,6 +73,224 @@
     return lax.psum_scatter(
         values.astype(BF16), G_AXES, scatter_dimension=0, tiled=True
     ).astype(F32)
+
+
+def meet(peers):
+    barrier = pltpu.get_barrier_semaphore()
+    for peer in peers:
+        pl.semaphore_signal(barrier, inc=1, device_id=peer, device_id_type=MESH)
+    pl.semaphore_wait(barrier, len(peers))
+
+
+def remote(src, dst, send, recv, peer):
+    return pltpu.make_async_remote_copy(
+        src_ref=src, dst_ref=dst, send_sem=send, recv_sem=recv, device_id=peer, device_id_type=MESH
+    )
+
+
+def group_place():
+    b1, b0, v = (lax.axis_index(axis) for axis in G_AXES)
+    chips = [((b1 + (d >> 1)) % 2, (v + (d & 1)) % 2) for d in range(4)]
+    peers = [{"b1": c1, "b0": b0, "v": cv} for c1, cv in chips]
+    partner = {"b1": b1, "b0": 1 - b0, "v": v}
+    return b0, chips, peers, partner
+
+
+def member(c1, b0, cv):
+    return (c1 * 2 + b0) * GV + cv
+
+
+def gather_kernel(x_ref, out_ref, send, recv, pass_send, pass_recv):
+    b0, chips, peers, partner = group_place()
+    mine = [member(c1, b0, cv) for c1, cv in chips]
+    meet([partner, *peers[1:]])
+    first = {}
+    for d in (3, 1, 2, 0):
+        first[d] = remote(
+            x_ref, out_ref.at[mine[0]], send.at[d], recv.at[d], peers[d] if d else partner
+        )
+        first[d].start()
+    out_ref[mine[0]] = x_ref[...]
+    passed = []
+    for d in (1, 2, 3):
+        first[d].wait_recv()
+        block = out_ref.at[mine[d]]
+        copy = remote(block, block, pass_send.at[d - 1], pass_recv.at[d - 1], partner)
+        copy.start()
+        passed.append(copy)
+    first[0].wait_recv()
+    for copy in first.values():
+        copy.wait_send()
+    for copy in passed:
+        copy.wait()
+
+
+def scatter_kernel(
+    y_ref, out_ref, came, total, arrived, send, recv, chip_send, chip_recv
+):
+    b0, chips, peers, partner = group_place()
+    meet([partner, *peers[1:]])
+    pair = {}
+    for d in (3, 1, 2, 0):
+        pair[d] = remote(
+            y_ref.at[member(chips[d][0], 1 - b0, chips[d][1])],
+            came.at[d],
+            send.at[d],
+            recv.at[d],
+            partner,
+        )
+        pair[d].start()
+    sent = {}
+    for d in (3, 1, 2):
+        pair[d].wait_recv()
+        own = y_ref[member(chips[d][0], b0, chips[d][1])].astype(F32)
+        total[d - 1] = (own + came[d].astype(F32)).astype(BF16)
+        sent[d] = remote(
+            total.at[d - 1], arrived.at[d - 1], chip_send.at[d - 1], chip_recv.at[d - 1], peers[d]
+        )
+        sent[d].start()
+    pair[0].wait_recv()
+    out_ref[...] = y_ref[member(chips[0][0], b0, chips[0][1])].astype(F32) + came[0].astype(F32)
+    for d in (1, 2, 3):
+        sent[d].wait_recv()
+        out_ref[...] += arrived[d - 1].astype(F32)
+    for d in range(4):
+        pair[d].wait_send()
+    for d in (1, 2, 3):
+        sent[d].wait_send()
+
+
+def call(kernel, out_shape, scratch, collective_id, cost, *args):
+    many = isinstance(out_shape, tuple)
+    return pl.pallas_call(
+        kernel,
+        out_shape=out_shape,
+        in_specs=[VMEM] * len(args),
+        out_specs=(VMEM,) * len(out_shape) if many else VMEM,
+        scratch_shapes=scratch,
+        cost_estimate=pl.CostEstimate(flops=0, bytes_accessed=cost, transcendentals=0),
+        compiler_params=pltpu.CompilerParams(
+            collective_id=collective_id, has_side_effects=True, vmem_limit_bytes=24 << 20
+        ),
+    )(*args)
+
+
+def dma(n):
+    return pltpu.SemaphoreType.DMA((n,))
+
+
+def gather_now(values):
+    rows, width = values.shape
+    out = jax.ShapeDtypeStruct((G, rows, width), values.dtype)
+    scratch = [dma(4), dma(4), dma(3), dma(3)]
+    return call(gather_kernel, out, scratch, 0, 32 << 20, values).reshape(G * rows, width)
+
+
+def scatter_now(values):
+    rows, width = values.shape[0] // G, values.shape[1]
+    block = (rows, width)
+    scratch = [
+        pltpu.VMEM((4, *block), BF16),
+        pltpu.VMEM((3, *block), BF16),
+        pltpu.VMEM((3, *block), BF16),
+        dma(4),
+        dma(4),
+        dma(3),
+        dma(3),
+    ]
+    out = jax.ShapeDtypeStruct(block, F32)
+    return call(
+        scatter_kernel, out, scratch, 1, 32 << 20, values.astype(BF16).reshape(G, *block)
+    )
+
+
+def shard_peers(shards):
+    me = (lax.axis_index("a") * 2 + lax.axis_index("b1")) * 2 + lax.axis_index("b0")
+    flats = [(me + k) % shards for k in range(shards)]
+    peers = [{"a": f // GB, "b1": (f // 2) % 2, "b0": f % 2} for f in flats]
+    return flats, peers
+
+
+def start_kernel(shards, p_ref, s_ref, all_ref, seg_ref, send, recv, seg_send, seg_recv):
+    flats, peers = shard_peers(shards)
+    b1, b0, v = (lax.axis_index(axis) for axis in G_AXES)
+    me = member(b1, b0, v)
+    others = [(me + k) % G for k in range(G)]
+    group = [{"b1": o // 4, "b0": (o // 2) % 2, "v": o % 2} for o in others]
+    meet([*peers[1:], *group[1:]])
+    copies = []
+    for k in range(1, shards):
+        copies.append(remote(p_ref, all_ref.at[flats[0]], send.at[k], recv.at[k], peers[k]))
+        copies[-1].start()
+    for k in range(1, G):
+        copies.append(remote(s_ref, seg_ref.at[me], seg_send.at[k], seg_recv.at[k], group[k]))
+        copies[-1].start()
+    all_ref[flats[0]] = p_ref[...]
+    seg_ref[me] = s_ref[...]
+    for copy in copies:
+        copy.wait()
+
+
+def start_now(small, segments, shards):
+    small = small.astype(F32).reshape(-1, 128)
+    segments = segments.astype(F32)
+    out = (
+        jax.ShapeDtypeStruct((shards, *small.shape), F32),
+        jax.ShapeDtypeStruct((G, *segments.shape), F32),
+    )
+    scratch = [dma(shards), dma(shards), dma(G), dma(G)]
+    kernel = functools.partial(start_kernel, shards)
+    params, segs = call(kernel, out, scratch, 2, 8 << 20, small, segments)
+    return params.reshape(shards, -1), segs[:, 0]
+
+
+def sums_kernel(shards, n_u, x_ref, out_ref, came, total, extra, send, recv, r_send, r_recv):
+    flats, peers = shard_peers(shards)
+    u, v = lax.axis_index("u"), lax.axis_index("v")
+    copies_n = n_u * GV
+    place = u * GV + v
+    twins = [(place + k) % copies_n for k in range(copies_n)]
+    twins = [{"u": t // GV, "v": t % GV} for t in twins]
+    meet([*peers[1:], *twins[1:]])
+    copies = []
+    for k in range(1, shards):
+        copies.append(
+            remote(x_ref.at[flats[k]], came.at[k], send.at[k], recv.at[k], peers[k])
+        )
+        copies[-1].start()
+    value = x_ref[flats[0]]
+    for k, copy in enumerate(copies, 1):
+        copy.wait_recv()
+        value += came[k]
+    total[...] = value
+    again = []
+    for k in range(1, copies_n):
+        again.append(remote(total, extra.at[k], r_send.at[k], r_recv.at[k], twins[k]))
+        again[-1].start()
+    for k, copy in enumerate(again, 1):
+        copy.wait_recv()
+        value += extra[k]
+    out_ref[...] = value
+    for copy in [*copies, *again]:
+        copy.wait_send()
+
+
+def sums_now(values, n_u):
+    shards, n = values.shape
+    values = values.reshape(shards, n // 128, 128)
+    block = values.shape[1:]
+    scratch = [
+        pltpu.VMEM((shards, *block), F32),
+        pltpu.VMEM(block, F32),
+        pltpu.VMEM((n_u * GV, *block), F32),
+        dma(shards),
+        dma(shards),
+        dma(n_u * GV),
+        dma(n_u * GV),
+    ]
+    out = jax.ShapeDtypeStruct(block, F32)
+    kernel = functools.partial(sums_kernel, shards, n_u)
+    return call(kernel, out, scratch, 3, 8 << 20, values).reshape(n)
 
 
 def on_device(
@@ -88,11 +313,12 @@
 ):
     rows, width = tokens.shape
     n_a = lax.axis_size("a")
-    n_bl = lax.axis_size("bl")
-    n_bh = lax.axis_size("bh")
     n_u = lax.axis_size("u")
     shards = n_a * GB
     depth = width // shards
+    n_bl = max(1, HEAD // depth)
+    n_bh = GB // n_bl
+    row_axes = ("a",) if n_bl == 1 else ("a", "b0")
     hidden_rows = fc_bias.shape[0]
     hidden = hidden_rows * shards
     half = hidden_rows // GV
@@ -101,10 +327,8 @@
     cols = heads_here * HEAD
     scale = HEAD ** (-0.5)
     v = lax.axis_index("v")
-    bl = lax.axis_index("bl")
-    bh = lax.axis_index("bh")
-    b = bh * n_bl + bl
-    me = lax.axis_index("a") * GB + b
+    b = lax.axis_index("b1") * 2 + lax.axis_index("b0")
+    bl = b % n_bl
 
     small = jnp.concatenate(
         [
@@ -119,7 +343,7 @@
             fc_bias,
         ]
     )
-    small = lax.all_gather(small, S_AXES, axis=0).astype(F32)
+    small, segments = start_now(small, segment_ids, shards)
     gain1, shift1, bias_query, bias_value, bias_out, gain2, shift2, bias_proj = (
         small[:, i * depth : (i + 1) * depth].reshape(width) for i in range(8)
     )
@@ -139,7 +363,7 @@
     qkv = lax.all_to_all(qkv, B_AXES, 0, 0, tiled=True).reshape(GB * depth, 3 * cols)
     fc = lax.all_to_all(fc, B_AXES, 0, 0, tiled=True).reshape(GB * depth, my_hidden)
     w_qkv = lax.all_gather(qkv, "a", axis=0, tiled=True)
-    w_out = lax.all_gather(out_weight, ("a", "bl"), axis=0, tiled=True)
+    w_out = lax.all_gather(out_weight, row_axes, axis=0, tiled=True)
     slot = bl * GV + v
     w_out = lax.dynamic_slice_in_dim(w_out, slot * cols, cols, 0)
     w_fc = lax.all_gather(fc, "a", axis=0, tiled=True)
@@ -155,10 +379,9 @@
     b_fc = pick(pick(bias_fc.reshape(n_a, GB, GV, half), b, 1), v, 1).reshape(my_hidden)
 
     cot_low = gather_group(cotangent.astype(BF16))
-    segments = lax.all_gather(segment_ids[0], G_AXES, axis=0)
 
     ln1, normed1, inv1 = layer_norm(tokens, gain1, shift1)
-    input1 = gather_group(ln1.astype(BF16))
+    input1 = gather_now(ln1.astype(BF16))
     blocks = GB * GV
     qkv_bias = jnp.concatenate([bq, jnp.zeros((cols,), F32), bv])
     projected = jnp.dot(input1, w_qkv, preferred_element_type=F32) + qkv_bias
@@ -177,17 +400,17 @@
     context = jnp.einsum("nhqk,nkhd->nqhd", probs_low, valued, preferred_element_type=F32)
     context = context.reshape(blocks * rows, cols).astype(BF16)
     middle = (
-        tokens + scatter_group(jnp.dot(context, w_out, preferred_element_type=F32)) + bias_out
+        tokens + scatter_now(jnp.dot(context, w_out, preferred_element_type=F32)) + bias_out
     )
 
     ln2, normed2, inv2 = layer_norm(middle, gain2, shift2)
-    input2 = gather_group(ln2.astype(BF16))
+    input2 = gather_now(ln2.astype(BF16))
     pre_act = jnp.dot(input2, w_fc, preferred_element_type=F32) + b_fc
     gelu_value, gelu_slope = gelu_pair(pre_act)
     activated = gelu_value.astype(BF16)
     grad_pre = contract(cot_low, w_proj, 1, 1) * gelu_slope
     grad_pre_low = grad_pre.astype(BF16)
-    grad_in2 = scatter_group(contract(grad_pre_low, w_fc, 1, 1))
+    grad_in2 = scatter_now(contract(grad_pre_low, w_fc, 1, 1))
     output = (
         middle + scatter_group(jnp.dot(activated, w_proj, preferred_element_type=F32)) + bias_proj
     )
@@ -213,7 +436,7 @@
     grad_shift2 = jnp.sum(grad_in2, axis=0)
     grad_middle = cotangent + norm_back(grad_in2, normed2, inv2, gain2)
 
-    mid_low = gather_group(grad_middle.astype(BF16))
+    mid_low = gather_now(grad_middle.astype(BF16))
     grad_out_weight = contract(context, mid_low, 0, 0)
     grad_context = contract(mid_low, w_out, 1, 1)
     grad_context = grad_context.astype(BF16).reshape(blocks, rows, heads_here, HEAD)
@@ -229,7 +452,7 @@
     grad_query_bias = jnp.sum(grad_query, axis=0)
     grad_value_bias = jnp.sum(grad_value, axis=0)
     grad_qkv = jnp.concatenate([grad_query, grad_key, grad_value], axis=1).astype(BF16)
-    grad_in1 = scatter_group(contract(grad_qkv, w_qkv, 1, 1))
+    grad_in1 = scatter_now(contract(grad_qkv, w_qkv, 1, 1))
     grad_qkv_weight = contract(input1, grad_qkv, 0, 0)
 
     share_qkv = columns_home(grad_qkv_weight).reshape(
@@ -241,7 +464,7 @@
     out_full = lax.dynamic_update_slice_in_dim(
         out_full, grad_out_weight.astype(BF16), slot * cols, 0
     )
-    share_out = lax.psum(reduce_a(out_full, ("a", "bl")), "v").astype(F32)
+    share_out = lax.psum(reduce_a(out_full, row_axes), "v").astype(F32)
 
     grad_gain1 = jnp.sum(grad_in1 * normed1, axis=0)
     grad_shift1 = jnp.sum(grad_in1, axis=0)
@@ -267,7 +490,7 @@
     ]
     sums = [s.reshape(shards, depth) for s in sums]
     sums = jnp.concatenate([*sums, fc_full.reshape(shards, hidden_rows)], axis=1)
-    sums = pick(lax.psum(sums, ALL_AXES), me, 0)
+    sums = sums_now(sums, n_u)
     (
         share_proj_bias,
         share_gain2,
@@ -300,11 +523,7 @@
 
 def solution(mesh):
     shard, replica = mesh.shape["shard"], mesh.shape["replica"]
-    head_parts = max(1, HEAD * shard // (HEADS * HEAD))
-    grid = mesh.devices.reshape(
-        shard // GB, GB // head_parts, head_parts, replica // GV, GV
-    )
-    inner = Mesh(grid, ALL_AXES)
+    inner = Mesh(mesh.devices.reshape(shard // GB, 2, 2, replica // GV, GV), ALL_AXES)
     row = P(ALL_AXES, None)
     vec = P(S_AXES)
     mat = P(S_AXES, None)

time: 568 us -> 359 us (0.63)
  waiting for transfers between devices: 285 us -> 43.2 us
  Pallas kernels: 0 us -> 120 us
  blocking collectives: 142 us -> 74.9 us
  matrix products: 50.8 us -> 42.8 us
  other arithmetic: 17.9 us -> 11.9 us
    pallas_call x0 -> x8, Pallas kernels: none -> 120 us  [call(): pl.pallas_call(kernel, out_shape=out_shape, in_specs=[VMEM] * len(args),...]
    reduce_scatter x4 -> x1, waiting for transfers between devices: 130 us -> 15.4 us  [scatter_group(): lax.psum_scatter(values.astype(BF16), G_AXES, scatter_dimension=0, tiled=...]
    all_gather x4 -> x1, waiting for transfers between devices: 83.4 us -> 0.01 us  [gather_group(): return lax.all_gather(values, G_AXES, axis=0, tiled=True)]
    psum x1 -> x0, blocking collectives: 39.7 us -> none  [on_device(): sums = pick(lax.psum(sums, ALL_AXES), me, 0)]
    all_gather x3 -> x1, blocking collectives: 52.7 us -> 20.1 us  [on_device(): w_out = lax.all_gather(out_weight, row_axes, axis=0, tiled=True)]
    reduce_scatter x4, waiting for transfers between devices: 41.8 us -> 10.2 us  [reduce_a(): lax.psum_scatter(values.astype(BF16), axes, scatter_dimension=0, tiled=True)]
    all_gather x1, waiting for transfers between devices: 25.6 us -> 0.01 us  [on_device(): lax.all_gather(lax.dynamic_slice_in_dim(proj_weight, v * half, half, 0),...]
    psum x1, waiting for transfers between devices: 0.01 us -> 12 us  [on_device(): share_out = lax.psum(reduce_a(out_full, row_axes), 'v').astype(F32)]
  transfers between devices with their start and end apart: 18 -> 12, of which waited for: 12 -> 4; matrix products, arithmetic and copies ran while one was open for 12% -> 23% of each run, Pallas kernels for 0% -> 34%
where the time goes in v2:
time: 359 us
  Pallas kernels  120 us (33%)
  blocking collectives  74.9 us (21%)
  waiting for transfers between devices  43.2 us (12%)
  matrix products  42.8 us (12%)
  local copies, waits for them, and re-layouts  39.8 us (11%)
  between operations  14.8 us (4%)
  other arithmetic  11.9 us (3%)
  starting transfers between devices  11 us (3%)
    pallas_call x8, Pallas kernels, call(): pl.pallas_call(kernel, out_shape=out_shape, in_specs=[VMEM] * len(args),...  120 us
    all_gather x1, blocking collectives, on_device(): w_qkv = lax.all_gather(qkv, 'a', axis=0, tiled=True)  21.3 us
    dot_general x8, matrix products, contract(): lax.dot_general(left, right, (((left_axis,), (right_axis,)), ((), ())), p...  20.5 us
    all_gather x1, blocking collectives, on_device(): w_out = lax.all_gather(out_weight, row_axes, axis=0, tiled=True)  20.1 us
    reduce_scatter x1, waiting for transfers between devices, scatter_group(): lax.psum_scatter(values.astype(BF16), G_AXES, scatter_dimension=0, tiled=...  15.4 us
    all_gather x2, blocking collectives, columns_home(): return lax.all_gather(values, 'v', axis=0)  13.9 us
    psum x1, waiting for transfers between devices, on_device(): share_out = lax.psum(reduce_a(out_full, row_axes), 'v').astype(F32)  12 us
    reduce_scatter x4, waiting for transfers between devices, reduce_a(): lax.psum_scatter(values.astype(BF16), axes, scatter_dimension=0, tiled=True)  10.2 us
  transfers between devices with their start and end apart: 12, of which 4 were waited for; matrix products, arithmetic and copies ran while one was open for 23% of the time, Pallas kernels for 34%

profile of v2, /device:TPU:0, one launch (start us, length us, event | category | flops | bytes accessed | tf_op | source)
XLA Modules:
  0.0 358.5 jit_solution(5460745332145236076)
XLA Ops:
  9.4 10.2 %all_to_all.20 = bf16[4,64,512]{2,1,0:T(8,128)(2,1)} all-to-all(bf16[4,64,512]{2,1,0:T(8,128)(2,1)S(1)} %copy_bitcast_fusion.1), channel_id=1, replica_groups=mesh['a'=4,'b1'=2,'b0'=2,'u'=1,'v'=2] {'b1','b0'}, dimensions={0} | all-to-all | bytes 524288 | tf_op jit(solution)/shard_map/all_to_all | solution.py:364
  23.3 3.4 all-to-all-start
  28.4 9.6 %shard_map.271 = (f32[16,6,128]{2,1,0:T(8,128)S(1)}, f32[8,1,128]{2,1,0:T(1,128)S(1)}) custom-call(f32[6,128]{1,0:T(8,128)S(1)} %bitcast_convert_fusion.p_ref, f32[1,128]{1,0:T(1,128)S(1)} %convert_element_type.124.s_ref), custom_call_target="tpu_custom_call" | custom-call | bytes 8388608 | tf_op jit(solution)/shard_map/pallas_call | solution.py:165
  38.8 20.1 %all_gather.31 = bf16[256,1024]{1,0:T(8,128)(2,1)} all-gather(bf16[64,1024]{1,0:T(8,128)(2,1)S(1)} %copy-done.21), channel_id=1, replica_groups=mesh['a'=4,'b1'=2,'b0'=2,'u'=1,'v'=2] {'a'}, dimensions={0}, use_global_device_ids=true | all-gather | bytes 655360 | tf_op jit(solution)/shard_map/all_gather | solution.py:366
  59.9 16.0 %shard_map.272 = bf16[8,128,1024]{2,1,0:T(8,128)(2,1)S(1)} custom-call(bf16[128,1024]{1,0:T(8,128)(2,1)S(1)} %add_convert_fusion.2.x_ref), custom_call_target="tpu_custom_call" | custom-call | bytes 33554432 | tf_op jit(solution)/shard_map/pallas_call | solution.py:165
  77.4 21.3 %all_gather.30 = bf16[1024,384]{1,0:T(8,128)(2,1)S(1)} all-gather(bf16[256,384]{1,0:T(8,128)(2,1)S(1)} %bitcast.169), channel_id=1, replica_groups=mesh['a'=4,'b1'=2,'b0'=2,'u'=1,'v'=2] {'a'}, dimensions={0}, use_global_device_ids=true | all-gather | bytes 983040 | tf_op jit(solution)/shard_map/all_gather | solution.py:365
  101.7 4.0 %reshape.320 = bf16[8,128,3,2,64]{4,3,2,1,0:T(2,128)(2,1)} reshape(bf16[1024,384]{1,0:T(8,128)(2,1)} %add_convert_fusion) | data formatting | bytes 1572864 | tf_op jit(solution)/shard_map/reshape | solution.py:388
  105.7 2.7 fusion.54
  111.6 17.7 %shard_map.273 = f32[128,1024]{1,0:T(8,128)S(1)} custom-call(bf16[8,128,1024]{2,1,0:T(8,128)(2,1)S(1)} %bitcast.150), custom_call_target="tpu_custom_call" | custom-call | bytes 33554432 | tf_op jit(solution)/shard_map/pallas_call | solution.py:165
  130.4 17.0 %shard_map.274 = bf16[8,128,1024]{2,1,0:T(8,128)(2,1)S(1)} custom-call(bf16[128,1024]{1,0:T(8,128)(2,1)S(1)} %add_convert_fusion.1.x_ref), custom_call_target="tpu_custom_call" | custom-call | bytes 33554432 | tf_op jit(solution)/shard_map/pallas_call | solution.py:165
  147.5 3.8 %fusion.64 = f32[1024,512]{1,0:T(8,128)} fusion(bf16[1024,1024]{1,0:T(8,128)(2,1)S(1)} %bitcast.155, bf16[1024,512]{1,0:T(8,128)(2,1)} %all-gather.6.cloned.1.call-done), kind=kOutput, calls=%fused_computation.125 | convolution fusion | flops 1073741824 | bytes 5242880 | tf_op jit(solution)/shard_map/dot_general | solution.py:408
  151.3 4.7 %convolution_convert_fusion.2 = bf16[1024,1024]{1,0:T(8,128)(2,1)} fusion(bf16[512,1024]{1,0:T(8,128)(2,1)} %all-gather.8.cloned.1.call-done, f32[1024,512]{1,0:T(8,128)} %fusion.64, f32[512]{0:T(512)S(1)} %bitcast.187), kind=kOutput, calls=%fused_computation.12 | convolution fusion | flops 1080033280 | bytes 5244928 | tf_op jit(solution)/shard_map/dot_general | solution.py:415
  156.3 5.0 %fusion.63 = (f32[512]{0:T(512)S(1)}, bf16[1024,512]{1,0:T(8,128)(2,1)S(1)}) fusion(f32[1024,512]{1,0:T(8,128)} %fusion.64, f32[512]{0:T(512)S(1)} %bitcast.188, bf16[512,1024]{1,0:T(8,128)(2,1)} %all-gather.8.cloned.1.call-done, bf16[1024,1024]{1,0:T(8,128)(2,1)} %all-gather.10.cloned.1.call-done), kind=kOutput, calls=%fused_computation.124 | convolution fusion | flops 1084751360 | bytes 6295552 | tf_op jit(solution)/shard_map/dot_general | solution.py:59
  162.7 16.6 %shard_map.275 = f32[128,1024]{1,0:T(8,128)S(1)} custom-call(bf16[8,128,1024]{2,1,0:T(8,128)(2,1)S(1)} %bitcast.152), custom_call_target="tpu_custom_call" | custom-call | bytes 33554432 | tf_op jit(solution)/shard_map/pallas_call | solution.py:165
  179.6 2.3 convolution_convert_fusion.5
  182.0 15.4 %reduce-scatter.6.cloned.1.call-done = bf16[128,1024]{1,0:T(8,128)(2,1)} async-done(((bf16[1024,1024]{1,0:T(8,128)(2,1)}), bf16[128,1024]{1,0:T(8,128)(2,1)}) %reduce-scatter.6.cloned.1.call-update) | async-done | bytes 262160 | tf_op jit(solution)/shard_map/reduce_scatter | solution.py:73
  200.5 16.6 %shard_map.276 = bf16[8,128,1024]{2,1,0:T(8,128)(2,1)S(1)} custom-call(bf16[128,1024]{1,0:T(8,128)(2,1)S(1)} %convert_element_type.139.x_ref), custom_call_target="tpu_custom_call" | custom-call | bytes 33554432 | tf_op jit(solution)/shard_map/pallas_call | solution.py:165
  225.8 3.6 %fusion.14 = bf16[8,128,2,64]{1,3,2,0:T(8,128)(2,1)} fusion(f32[8,2,128,128]{2,3,1,0:T(8,128)} %fusion.34, f32[8,2,128,128]{2,3,1,0:T(8,128)} %copy-done.5, f32[8,2,128]{2,1,0:T(2,128)S(1)} %bitcast.176, bf16[8,128,1,2,64]{1,4,3,0,2:T(8,128)(2,1)} %copy-done.16), kind=kOutput, calls=%fused_computation.32 | convolution fusion | flops 35522688 | bytes 2629632 | tf_op jit(solution)/shard_map/nhqk,nqhd->nkhd/dot_general | solution.py:448
  230.6 3.5 fusion.56
  238.7 4.6 %convolution_convert_fusion.4 = bf16[512,1024]{1,0:T(8,128)(2,1)} fusion(bf16[1024,1024]{1,0:T(8,128)(2,1)} %all-gather.10.cloned.1.call-done, f32[1024,512]{1,0:T(8,128)} %fusion.64, f32[512]{0:T(512)S(1)} %bitcast.189), kind=kOutput, calls=%fused_computation.15 | convolution fusion | flops 1079508992 | bytes 5244928 | tf_op jit(solution)/shard_map/dot_general | solution.py:59
  245.3 2.4 convolution_convert_fusion
  247.8 16.5 %shard_map.277 = f32[128,1024]{1,0:T(8,128)S(1)} custom-call(bf16[8,128,1024]{2,1,0:T(8,128)(2,1)S(1)} %bitcast.151), custom_call_target="tpu_custom_call" | custom-call | bytes 33554432 | tf_op jit(solution)/shard_map/pallas_call | solution.py:165
  265.6 10.1 %shard_map.278 = f32[6,128]{1,0:T(8,128)S(1)} custom-call(f32[16,6,128]{2,1,0:T(8,128)S(1)} %reshape.305.x_ref), custom_call_target="tpu_custom_call" | custom-call | bytes 8388608 | tf_op jit(solution)/shard_map/pallas_call | solution.py:165
  281.2 3.4 all-to-all-start.3
  285.2 5.4 %all-to-all-done.3 = bf16[4,64,512]{2,1,0:T(8,128)(2,1)S(1)} async-done(((bf16[4,64,512]{2,1,0:T(8,128)(2,1)}), bf16[4,64,512]{2,1,0:T(8,128)(2,1)S(1)}, u32[]{:S(2)}, u32[]{:S(2)}) %all-to-all-start.3) | async-done | bytes 262176 | tf_op jit(solution)/shard_map/all_to_all | solution.py:429
  290.6 3.4 all-to-all-start.2
  294.1 9.5 %all_gather.39 = bf16[256,1024]{1,0:T(8,128)(2,1)S(1)} all-gather(bf16[128,1024]{1,0:T(8,128)(2,1)} %reduce-scatter.14.cloned.1.call-done), channel_id=1, replica_groups=mesh['a'=4,'b1'=2,'b0'=2,'u'=1,'v'=2] {'v'}, dimensions={0}, use_global_device_ids=true | all-gather | bytes 786432 | tf_op jit(solution)/shard_map/all_gather | solution.py:425
  304.6 10.2 %reduce-scatter.10.cloned.1.call-done = bf16[64,1024]{1,0:T(8,128)(2,1)} async-done(((bf16[256,1024]{1,0:T(8,128)(2,1)}), bf16[64,1024]{1,0:T(8,128)(2,1)}) %reduce-scatter.10.cloned.1.call-update) | async-done | bytes 131088 | tf_op jit(solution)/shard_map/reduce_scatter | solution.py:422
  314.8 7.0 %all-gather.1 = bf16[8,64,512]{2,1,0:T(8,128)(2,1)S(1)} all-gather(bf16[4,64,512]{2,1,0:T(8,128)(2,1)S(1)} %all-to-all-done.3), channel_id=3, replica_groups=mesh['a'=4,'b1'=2,'b0'=2,'u'=1,'v'=2] {'v'}, dimensions={0}, use_global_device_ids=true | all-gather | bytes 786432 | tf_op jit(solution)/shard_map/all_gather | solution.py:430
  324.9 12.0 %all-reduce.2.cloned.1.call-done = bf16[64,1024]{1,0:T(8,128)(2,1)} async-done(((bf16[64,1024]{1,0:T(8,128)(2,1)}), bf16[64,1024]{1,0:T(8,128)(2,1)}) %all-reduce.2.cloned.1.call-update) | async-done | bytes 131088 | tf_op jit(solution)/shard_map/psum | solution.py:467
  338.5 6.9 %all-gather = bf16[8,64,384]{2,1,0:T(8,128)(2,1)S(1)} all-gather(bf16[4,64,384]{2,1,0:T(8,128)(2,1)S(1)} %all-to-all-done.2), channel_id=2, replica_groups=mesh['a'=4,'b1'=2,'b0'=2,'u'=1,'v'=2] {'v'}, dimensions={0}, use_global_device_ids=true | all-gather | bytes 589824 | tf_op jit(solution)/shard_map/all_gather | solution.py:430
  347.6 2.4 copy.118
  (216 shorter events, 56.3 us)
Async XLA Ops:
  7.2 12.5 %copy-start = (bf16[256,1024]{1,0:T(8,128)(2,1)S(1)}, bf16[256,1024]{1,0:T(8,128)(2,1)}, u32[]{:S(2)}) copy-start(bf16[256,1024]{1,0:T(8,128)(2,1)} %param.30) | copy-start | bytes 1572868
  7.2 140.3 %all-gather.6.cloned.1.call-start = ((), (), s32[]{:S(2)}) async-start(), calls=%async_computation.9 | async-start | bytes 1310720 | tf_op jit(solution)/shard_map/all_gather | solution.py:369
  7.2 13.2 %copy-start.20 = (bf16[64,3072]{1,0:T(8,128)(2,1)S(1)}, bf16[64,3072]{1,0:T(8,128)(2,1)}, u32[]{:S(2)}) copy-start(bf16[64,3072]{1,0:T(8,128)(2,1)} %param.21) | copy-start | bytes 1179652
  19.6 131.6 %all-gather.8.cloned.1.call-start = ((), (), s32[]{:S(2)}) async-start(), calls=%async_computation.10 | async-start | bytes 1310720 | tf_op jit(solution)/shard_map/all_gather | solution.py:370
  21.9 16.5 %copy-start.3 = (f32[128,1024]{1,0:T(8,128)S(1)}, f32[128,1024]{1,0:T(8,128)}, u32[]{:S(2)}) copy-start(f32[128,1024]{1,0:T(8,128)} %param.16) | copy-start | bytes 1572868
  22.2 16.5 %copy-start.21 = (bf16[64,1024]{1,0:T(8,128)(2,1)S(1)}, bf16[64,1024]{1,0:T(8,128)(2,1)}, u32[]{:S(2)}) copy-start(bf16[64,1024]{1,0:T(8,128)(2,1)} %param.24) | copy-start | bytes 393220
  23.3 54.0 %all-to-all-start = ((bf16[4,64,384]{2,1,0:T(8,128)(2,1)}), bf16[4,64,384]{2,1,0:T(8,128)(2,1)S(1)}, u32[]{:S(2)}, u32[]{:S(2)}) async-start(bf16[4,64,384]{2,1,0:T(8,128)(2,1)} %reshape.283), calls=%async_computation | async-start | bytes 393216 | tf_op jit(solution)/shard_map/all_to_all | solution.py:363
  26.7 129.7 %all-gather.10.cloned.1.call-start = ((), (), s32[]{:S(2)}) async-start(), calls=%async_computation.12 | async-start | bytes 2359296 | tf_op jit(solution)/shard_map/all_gather | solution.py:69
  28.1 169.3 %reduce-scatter.6.cloned.1.call-start = ((), (), s32[]{:S(2)}) async-start(), calls=%async_computation.11 | async-start | bytes 2359296 | tf_op jit(solution)/shard_map/reduce_scatter | solution.py:73
  38.5 37.3 %copy-start.28 = (f32[128]{0:T(128)}, f32[128]{0:T(128)S(1)}, u32[]{:S(2)}) copy-start(f32[128]{0:T(128)S(1)} %broadcast_multiply_fusion.8) | copy-start | bytes 1540
  38.8 59.9 %copy-start.30 = (f32[128]{0:T(128)}, f32[128]{0:T(128)S(1)}, u32[]{:S(2)}) copy-start(f32[128]{0:T(128)S(1)} %add_rsqrt_fusion.1) | copy-start | bytes 1540
  75.8 25.8 %copy-start.1 = (bf16[8,128,1024]{2,1,0:T(8,128)(2,1)}, bf16[8,128,1024]{2,1,0:T(8,128)(2,1)S(1)}, u32[]{:S(2)}) copy-start(bf16[8,128,1024]{2,1,0:T(8,128)(2,1)S(1)} %shard_map.272) | copy-start | bytes 6291460
  110.8 18.5 %copy-start.9 = (bf16[8,128,2,64]{1,0,3,2:T(8,128)(2,1)}, bf16[8,128,2,64]{1,0,3,2:T(8,128)(2,1)S(1)}, u32[]{:S(2)}) copy-start(bf16[8,128,2,64]{1,0,3,2:T(8,128)(2,1)S(1)} %copy.104) | copy-start | bytes 786436
  110.8 18.5 %copy-start.27 = (f32[1024]{0:T(1024)S(1)}, f32[1024]{0:T(1024)}, u32[]{:S(2)}) copy-start(f32[1024]{0:T(1024)} %add.180) | copy-start | bytes 12292
  111.6 18.7 %copy-start.26 = (f32[1024]{0:T(1024)S(1)}, f32[1024]{0:T(1024)}, u32[]{:S(2)}) copy-start(f32[1024]{0:T(1024)} %add.184) | copy-start | bytes 12292
  156.0 125.2 %reduce-scatter.12.cloned.1.call-start = ((), (), s32[]{:S(2)}) async-start(), calls=%async_computation.16 | async-start | bytes 1310720 | tf_op jit(solution)/shard_map/reduce_scatter | solution.py:422
  162.7 16.6 %copy-start.7 = (f32[128,1024]{1,0:T(8,128)S(1)}, f32[128,1024]{1,0:T(8,128)}, u32[]{:S(2)}) copy-start(f32[128,1024]{1,0:T(8,128)} %copy-done.6) | copy-start | bytes 1572868
  182.0 108.6 %reduce-scatter.8.cloned.1.call-start = ((), (), s32[]{:S(2)}) async-start(), calls=%async_computation.13 | async-start | bytes 983040 | tf_op jit(solution)/shard_map/reduce_scatter | solution.py:422
  199.7 17.5 %copy-start.13 = (bf16[256,1024]{1,0:T(8,128)(2,1)S(1)}, bf16[256,1024]{1,0:T(8,128)(2,1)}, u32[]{:S(2)}) copy-start(bf16[256,1024]{1,0:T(8,128)(2,1)} %all_gather.31) | copy-start | bytes 1572868
  238.7 6.6 %copy-start.19 = (bf16[1024,384]{1,0:T(8,128)(2,1)S(1)}, bf16[1024,384]{1,0:T(8,128)(2,1)}, u32[]{:S(2)}) copy-start(bf16[1024,384]{1,0:T(8,128)(2,1)} %copy-done.18) | copy-start | bytes 2359300
  238.7 55.4 %reduce-scatter.14.cloned.1.call-start = ((), (), s32[]{:S(2)}) async-start(), calls=%async_computation.17 | async-start | bytes 1310720 | tf_op jit(solution)/shard_map/reduce_scatter | solution.py:422
  243.4 71.4 %reduce-scatter.10.cloned.1.call-start = ((), (), s32[]{:S(2)}) async-start(), calls=%async_computation.14 | async-start | bytes 655360 | tf_op jit(solution)/shard_map/reduce_scatter | solution.py:422
  247.8 16.6 %copy-start.4 = (f32[128,1024]{1,0:T(8,128)S(1)}, f32[128,1024]{1,0:T(8,128)}, u32[]{:S(2)}) copy-start(f32[128,1024]{1,0:T(8,128)} %param.16) | copy-start | bytes 1572868
  247.8 16.6 %copy-start.29 = (f32[128]{0:T(128)S(1)}, f32[128]{0:T(128)}, u32[]{:S(2)}) copy-start(f32[128]{0:T(128)} %copy-done.28) | copy-start | bytes 1540
  247.8 16.6 %copy-start.31 = (f32[128]{0:T(128)S(1)}, f32[128]{0:T(128)}, u32[]{:S(2)}) copy-start(f32[128]{0:T(128)} %copy-done.30) | copy-start | bytes 1540
  247.8 17.7 %copy-start.23 = (f32[2,8,2,128]{3,1,2,0:T(8,128)S(1)}, f32[2,8,2,128]{3,1,2,0:T(8,128)}, u32[]{:S(2)}) copy-start(f32[2,8,2,128]{3,1,2,0:T(8,128)} %copy.158) | copy-start | bytes 49156
  247.8 17.7 %copy-start.24 = (f32[16,64]{1,0:T(8,128)S(1)}, f32[16,64]{1,0:T(8,128)}, u32[]{:S(2)}) copy-start(f32[16,64]{1,0:T(8,128)} %reshape.301) | copy-start | bytes 12292
  247.8 29.3 %copy-start.10 = (bf16[8,128,2,64]{1,0,3,2:T(8,128)(2,1)S(1)}, bf16[8,128,2,64]{1,0,3,2:T(8,128)(2,1)}, u32[]{:S(2)}) copy-start(bf16[8,128,2,64]{1,0,3,2:T(8,128)(2,1)} %copy-done.9) | copy-start | bytes 786436
  265.3 13.0 %copy-start.33 = (f32[128]{0:T(128)S(1)}, f32[128]{0:T(128)}, u32[]{:S(2)}) copy-start(f32[128]{0:T(128)} %get-tuple-element.24) | copy-start | bytes 1540
  281.2 9.4 %all-to-all-start.3 = ((bf16[4,64,512]{2,1,0:T(8,128)(2,1)}), bf16[4,64,512]{2,1,0:T(8,128)(2,1)S(1)}, u32[]{:S(2)}, u32[]{:S(2)}) async-start(bf16[4,64,512]{2,1,0:T(8,128)(2,1)} %bitcast.172), calls=%async_computation.7 | async-start | bytes 524288 | tf_op jit(solution)/shard_map/all_to_all | solution.py:429
  290.6 47.9 %all-to-all-start.2 = ((bf16[4,64,384]{2,1,0:T(8,128)(2,1)}), bf16[4,64,384]{2,1,0:T(8,128)(2,1)S(1)}, u32[]{:S(2)}, u32[]{:S(2)}) async-start(bf16[4,64,384]{2,1,0:T(8,128)(2,1)} %bitcast.173), calls=%async_computation.4 | async-start | bytes 393216 | tf_op jit(solution)/shard_map/all_to_all | solution.py:429
  294.0 42.9 %all-reduce.2.cloned.1.call-start = ((), (), s32[]{:S(2)}) async-start(), calls=%async_computation.15 | async-start | bytes 262144 | tf_op jit(solution)/shard_map/psum | solution.py:467
  (25 other events, 106.8 us)
Sparse Core Ops, SparseCore 0:
  19.7 36.2 all-gather.5
  58.2 30.2 all-gather.7
  90.9 35.2 all-gather.9
  156.1 41.2 reduce-scatter.5
  199.6 27.1 reduce-scatter.11
  238.8 23.1 reduce-scatter.7
  264.8 26.6 reduce-scatter.13
  294.5 20.3 reduce-scatter.9
  317.2 19.6 all-reduce.1

commit v3 on v2

--- a/solution.py
+++ b/solution.py
@@ -211,86 +211,205 @@
     return flats, peers
 
 
-def start_kernel(shards, p_ref, s_ref, all_ref, seg_ref, send, recv, seg_send, seg_recv):
-    flats, peers = shard_peers(shards)
+def group_peers():
     b1, b0, v = (lax.axis_index(axis) for axis in G_AXES)
     me = member(b1, b0, v)
     others = [(me + k) % G for k in range(G)]
-    group = [{"b1": o // 4, "b0": (o // 2) % 2, "v": o % 2} for o in others]
-    meet([*peers[1:], *group[1:]])
+    return others, [{"b1": o // 4, "b0": (o // 2) % 2, "v": o % 2} for o in others]
+
+
+def start_kernel(
+    shards,
+    p_ref,
+    s_ref,
+    q_ref,
+    f_ref,
+    all_ref,
+    seg_ref,
+    q_all,
+    f_all,
+    send,
+    recv,
+    seg_send,
+    seg_recv,
+    q_send,
+    q_recv,
+    f_send,
+    f_recv,
+):
+    flats, peers = shard_peers(shards)
+    others, group = group_peers()
+    me, mine = flats[0], others[0]
+    b = me % GB
+    columns = [(b + k) % GB for k in range(GB)]
+    column_peers = [{"b1": o // 2, "b0": o % 2} for o in columns]
+    meet([*peers[1:], *group[1:], *column_peers[1:]])
     copies = []
     for k in range(1, shards):
-        copies.append(remote(p_ref, all_ref.at[flats[0]], send.at[k], recv.at[k], peers[k]))
-        copies[-1].start()
+        copies.append(remote(p_ref, all_ref.at[me], send.at[k], recv.at[k], peers[k]))
+        copies.append(
+            remote(q_ref.at[flats[k] % GB], q_all.at[me], q_send.at[k], q_recv.at[k], peers[k])
+        )
     for k in range(1, G):
-        copies.append(remote(s_ref, seg_ref.at[me], seg_send.at[k], seg_recv.at[k], group[k]))
-        copies[-1].start()
-    all_ref[flats[0]] = p_ref[...]
-    seg_ref[me] = s_ref[...]
+        copies.append(remote(s_ref, seg_ref.at[mine], seg_send.at[k], seg_recv.at[k], group[k]))
+    for k in range(1, GB):
+        copies.append(
+            remote(
+                f_ref.at[columns[k]], f_all.at[b], f_send.at[k], f_recv.at[k], column_peers[k]
+            )
+        )
+    for copy in copies:
+        copy.start()
+    all_ref[me] = p_ref[...]
+    seg_ref[mine] = s_ref[...]
+    q_all[me] = q_ref[b]
+    f_all[b] = f_ref[b]
     for copy in copies:
         copy.wait()
 
 
-def start_now(small, segments, shards):
+def start_now(small, segments, qkv, fc, shards):
     small = small.astype(F32).reshape(-1, 128)
     segments = segments.astype(F32)
     out = (
         jax.ShapeDtypeStruct((shards, *small.shape), F32),
         jax.ShapeDtypeStruct((G, *segments.shape), F32),
+        jax.ShapeDtypeStruct((shards, *qkv.shape[1:]), BF16),
+        jax.ShapeDtypeStruct(fc.shape, BF16),
     )
     scratch = [dma(shards), dma(shards), dma(G), dma(G)]
+    scratch += [dma(shards), dma(shards), dma(GB), dma(GB)]
     kernel = functools.partial(start_kernel, shards)
-    params, segs = call(kernel, out, scratch, 2, 8 << 20, small, segments)
-    return params.reshape(shards, -1), segs[:, 0]
-
-
-def sums_kernel(shards, n_u, x_ref, out_ref, came, total, extra, send, recv, r_send, r_recv):
+    params, segs, qkv, fc = call(kernel, out, scratch, 2, 32 << 20, small, segments, qkv, fc)
+    return params.reshape(shards, -1), segs[:, 0], qkv, fc
+
+
+def tail_kernel(
+    shards,
+    n_u,
+    x_ref,
+    q_ref,
+    f_ref,
+    p_ref,
+    o_ref,
+    x_out,
+    q_out,
+    f_out,
+    p_out,
+    o_out,
+    came,
+    total,
+    extra,
+    q_came,
+    q_total,
+    q_extra,
+    send,
+    recv,
+    q_send,
+    q_recv,
+    f_send,
+    f_recv,
+    t_send,
+    t_recv,
+    one_send,
+    one_recv,
+):
     flats, peers = shard_peers(shards)
+    others, group = group_peers()
+    me, mine = flats[0], others[0]
     u, v = lax.axis_index("u"), lax.axis_index("v")
-    copies_n = n_u * GV
-    place = u * GV + v
-    twins = [(place + k) % copies_n for k in range(copies_n)]
+    b = me % GB
+    twins_n = n_u * GV
+    twins = [(u * GV + v + k) % twins_n for k in range(twins_n)]
     twins = [{"u": t // GV, "v": t % GV} for t in twins]
-    meet([*peers[1:], *twins[1:]])
-    copies = []
+    other_v = {"v": 1 - v}
+    meet([*peers[1:], *group[1:], *twins[1:], other_v])
+    q_copies, copies, rest = [], [], []
     for k in range(1, shards):
-        copies.append(
-            remote(x_ref.at[flats[k]], came.at[k], send.at[k], recv.at[k], peers[k])
-        )
+        q_copies.append(
+            remote(q_ref.at[flats[k]], q_came.at[k], q_send.at[k], q_recv.at[k], peers[k])
+        )
+        q_copies[-1].start()
+    for k in range(1, shards):
+        copies.append(remote(x_ref.at[flats[k]], came.at[k], send.at[k], recv.at[k], peers[k]))
         copies[-1].start()
-    value = x_ref[flats[0]]
+    for k in range(1, G):
+        to = others[k] // GV
+        rest.append(
+            remote(f_ref.at[to], f_out.at[v * GB + b], f_send.at[k], f_recv.at[k], group[k])
+        )
+    rest.append(remote(p_ref, p_out.at[v], one_send.at[0], one_recv.at[0], other_v))
+    rest.append(remote(o_ref, o_out.at[v], one_send.at[1], one_recv.at[1], other_v))
+    for copy in rest:
+        copy.start()
+    f_out[v * GB + b] = f_ref[b]
+    p_out[v] = p_ref[...]
+    o_out[v] = o_ref[...]
+
+    for copy in q_copies:
+        copy.wait_recv()
+    for r in range(GB):
+        start = q_ref[me].astype(F32) if r == 0 else q_came[r].astype(F32)
+        for k in range(r + GB, shards, GB):
+            start += q_came[k].astype(F32)
+        q_total[(b + GB - r) % GB] = start.astype(BF16)
+    value = x_ref[me]
     for k, copy in enumerate(copies, 1):
         copy.wait_recv()
         value += came[k]
     total[...] = value
     again = []
-    for k in range(1, copies_n):
-        again.append(remote(total, extra.at[k], r_send.at[k], r_recv.at[k], twins[k]))
-        again[-1].start()
-    for k, copy in enumerate(again, 1):
+    for k in range(1, twins_n):
+        pair = (
+            remote(q_total, q_extra.at[k], t_send.at[k], t_recv.at[k], twins[k]),
+            remote(
+                total, extra.at[k], t_send.at[twins_n + k], t_recv.at[twins_n + k], twins[k]
+            ),
+        )
+        for copy in pair:
+            copy.start()
+        again += pair
+    for copy in again:
         copy.wait_recv()
+    for k in range(1, twins_n):
         value += extra[k]
-    out_ref[...] = value
-    for copy in [*copies, *again]:
+    x_out[...] = value
+    for side in range(GV):
+        first = q_total[...] if side == 0 else q_extra[side]
+        first = first.astype(F32)
+        for k in range(side + GV, twins_n, GV):
+            first += q_extra[k].astype(F32)
+        q_out[(v + side) % GV] = first
+    for copy in rest:
+        copy.wait()
+    for copy in [*q_copies, *copies, *again]:
         copy.wait_send()
 
 
-def sums_now(values, n_u):
-    shards, n = values.shape
-    values = values.reshape(shards, n // 128, 128)
-    block = values.shape[1:]
+def tail_now(sums, qkv, fc, proj, out, n_u):
+    shards, n = sums.shape
+    sums = sums.reshape(shards, n // 128, 128)
+    block, q_block = sums.shape[1:], qkv.shape[1:]
+    twins_n = n_u * GV
+    shapes = (
+        jax.ShapeDtypeStruct(block, F32),
+        jax.ShapeDtypeStruct((GV, GB, *q_block), F32),
+        jax.ShapeDtypeStruct((GV * GB, *fc.shape[1:]), BF16),
+        jax.ShapeDtypeStruct((GV, *proj.shape), BF16),
+        jax.ShapeDtypeStruct((GV, *out.shape), BF16),
+    )
     scratch = [
         pltpu.VMEM((shards, *block), F32),
         pltpu.VMEM(block, F32),
-        pltpu.VMEM((n_u * GV, *block), F32),
-        dma(shards),
-        dma(shards),
-        dma(n_u * GV),
-        dma(n_u * GV),
+        pltpu.VMEM((twins_n, *block), F32),
+        pltpu.VMEM((shards, *q_block), BF16),
+        pltpu.VMEM((GB, *q_block), BF16),
+        pltpu.VMEM((twins_n, GB, *q_block), BF16),
+        *(dma(n) for n in (shards, shards, shards, shards, G, G)),
+        *(dma(n) for n in (2 * twins_n, 2 * twins_n, 2, 2)),
     ]
-    out = jax.ShapeDtypeStruct(block, F32)
-    kernel = functools.partial(sums_kernel, shards, n_u)
-    return call(kernel, out, scratch, 3, 8 << 20, values).reshape(n)
+    kernel = functools.partial(tail_kernel, shards, n_u)
+    return call(kernel, shapes, scratch, 3, 32 << 20, sums, qkv, fc, proj, out)
 
 
 def on_device(
@@ -343,12 +462,6 @@
             fc_bias,
         ]
     )
-    small, segments = start_now(small, segment_ids, shards)
-    gain1, shift1, bias_query, bias_value, bias_out, gain2, shift2, bias_proj = (
-        small[:, i * depth : (i + 1) * depth].reshape(width) for i in range(8)
-    )
-    bias_fc = small[:, 8 * depth :]
-
     def head_split(values):
         lead = values.shape[:-1]
         n = len(lead)
@@ -360,16 +473,21 @@
     qkv = qkv.reshape(GB, depth, 3 * cols)
     fc = pick(fc_weight.reshape(depth, n_a, GB, GV, half), v, 3)
     fc = fc.transpose(2, 0, 1, 3).reshape(GB, depth, my_hidden)
-    qkv = lax.all_to_all(qkv, B_AXES, 0, 0, tiled=True).reshape(GB * depth, 3 * cols)
-    fc = lax.all_to_all(fc, B_AXES, 0, 0, tiled=True).reshape(GB * depth, my_hidden)
-    w_qkv = lax.all_gather(qkv, "a", axis=0, tiled=True)
+    small, segments, qkv, fc = start_now(small, segment_ids, qkv, fc, shards)
+    gain1, shift1, bias_query, bias_value, bias_out, gain2, shift2, bias_proj = (
+        small[:, i * depth : (i + 1) * depth].reshape(width) for i in range(8)
+    )
+    bias_fc = small[:, 8 * depth :]
+
+    w_qkv = qkv.reshape(width, 3 * cols)
     w_out = lax.all_gather(out_weight, row_axes, axis=0, tiled=True)
     slot = bl * GV + v
     w_out = lax.dynamic_slice_in_dim(w_out, slot * cols, cols, 0)
-    w_fc = lax.all_gather(fc, "a", axis=0, tiled=True)
-    w_proj = lax.all_gather(
-        lax.dynamic_slice_in_dim(proj_weight, v * half, half, 0), "a", axis=0, tiled=True
-    )
+    proj_half = lax.dynamic_slice_in_dim(proj_weight, v * half, half, 0)
+    both = jnp.concatenate([fc.reshape(-1, width), proj_half], axis=0)
+    both = lax.all_gather(both, "a", axis=0)
+    w_fc = both[:, :-half].reshape(width, my_hidden)
+    w_proj = both[:, -half:].reshape(my_hidden, width)
 
     def my_heads(values):
         return pick(head_split(values).reshape(GB, GV, cols), b, 0)
@@ -422,15 +540,8 @@
         values = lax.psum_scatter(values.astype(BF16), axes, scatter_dimension=0, tiled=True)
         return lax.psum(values, "u") if n_u > 1 else values
 
-    share_proj = lax.all_gather(reduce_a(grad_proj_weight), "v", axis=0, tiled=True).astype(F32)
-
-    def columns_home(values):
-        values = reduce_a(values).reshape(GB, depth, values.shape[1])
-        values = lax.all_to_all(values, B_AXES, 0, 0, tiled=True)
-        return lax.all_gather(values, "v", axis=0)
-
-    share_fc = columns_home(grad_fc_weight).reshape(GV, GB, depth, n_a, half)
-    share_fc = share_fc.transpose(2, 3, 1, 0, 4).reshape(depth, hidden).astype(F32)
+    part_proj = reduce_a(grad_proj_weight)
+    part_fc = reduce_a(grad_fc_weight).reshape(GB, depth, my_hidden)
 
     grad_gain2 = jnp.sum(grad_in2 * normed2, axis=0)
     grad_shift2 = jnp.sum(grad_in2, axis=0)
@@ -455,16 +566,11 @@
     grad_in1 = scatter_now(contract(grad_qkv, w_qkv, 1, 1))
     grad_qkv_weight = contract(input1, grad_qkv, 0, 0)
 
-    share_qkv = columns_home(grad_qkv_weight).reshape(
-        GV, n_bh, n_bl, depth, 3, heads_here, HEAD
-    )
-    share_qkv = share_qkv.transpose(3, 4, 2, 0, 5, 1, 6).reshape(depth, 3 * width).astype(F32)
-
     out_full = jnp.zeros((depth * n_a * n_bl, width), BF16)
     out_full = lax.dynamic_update_slice_in_dim(
         out_full, grad_out_weight.astype(BF16), slot * cols, 0
     )
-    share_out = lax.psum(reduce_a(out_full, row_axes), "v").astype(F32)
+    part_out = reduce_a(out_full, row_axes)
 
     grad_gain1 = jnp.sum(grad_in1 * normed1, axis=0)
     grad_shift1 = jnp.sum(grad_in1, axis=0)
@@ -490,7 +596,17 @@
     ]
     sums = [s.reshape(shards, depth) for s in sums]
     sums = jnp.concatenate([*sums, fc_full.reshape(shards, hidden_rows)], axis=1)
-    sums = sums_now(sums, n_u)
+    part_qkv = grad_qkv_weight.astype(BF16).reshape(shards, depth, 3 * cols)
+    sums, share_qkv, share_fc, share_proj, share_out = tail_now(
+        sums, part_qkv, part_fc, part_proj, part_out, n_u
+    )
+    sums = sums.reshape(-1)
+    share_qkv = share_qkv.reshape(GV, n_bh, n_bl, depth, 3, heads_here, HEAD)
+    share_qkv = share_qkv.transpose(3, 4, 2, 0, 5, 1, 6).reshape(depth, 3 * width)
+    share_fc = share_fc.reshape(GV, GB, depth, n_a, half)
+    share_fc = share_fc.transpose(2, 3, 1, 0, 4).reshape(depth, hidden).astype(F32)
+    share_proj = share_proj.reshape(hidden_rows, width).astype(F32)
+    share_out = share_out[0].astype(F32) + share_out[1].astype(F32)
     (
         share_proj_bias,
         share_gain2,

time: 359 us -> 340 us (0.947)
  blocking collectives: 74.9 us -> 25.7 us
  Pallas kernels: 120 us -> 157 us
  local copies, waits for them, and re-layouts: 39.8 us -> 60.6 us
  waiting for transfers between devices: 43.2 us -> 28.1 us
  starting transfers between devices: 11 us -> 0.25 us
  matrix products: 42.8 us -> 38.5 us
    all_gather x4 -> x0, blocking collectives: 44.7 us -> none  [the longest x1 21.3 us: on_device(): w_qkv = lax.all_gather(qkv, 'a', axis=0, tiled=True)]
    pallas_call x8, Pallas kernels: 120 us -> 157 us  [call(): pl.pallas_call(kernel, out_shape=out_shape, in_specs=[VMEM] * len(args),...]
    psum x1 -> x0, waiting for transfers between devices: 12 us -> none  [on_device(): share_out = lax.psum(reduce_a(out_full, row_axes), 'v').astype(F32)]
    all_to_all x1 -> x0, blocking collectives: 10.2 us -> none  [on_device(): lax.all_to_all(fc, B_AXES, 0, 0, tiled=True).reshape(GB * depth, my_hidden)]
    all_to_all x3 -> x0, starting transfers between devices: 10.1 us -> none  [the longest x2 6.77 us: columns_home(): values = lax.all_to_all(values, B_AXES, 0, 0, tiled=True)]
    reshape x2, local copies, waits for them, and re-layouts: 3.24 us -> 12.8 us  [on_device(): grad_context.astype(BF16).reshape(blocks, rows, heads_here, HEAD)]
    reshape x1 -> x5, local copies, waits for them, and re-layouts: 0.01 us -> 7.86 us  [the longest x1 3.4 us: on_device(): share_qkv.transpose(3, 4, 2, 0, 5, 1, 6).reshape(depth, 3 * width)]
    convert_element_type x3 -> x0, local copies, waits for them, and re-layouts: 6.64 us -> none  [on_device(): share_qkv.transpose(3, 4, 2, 0, 5, 1, 6).reshape(depth, 3 * width)]
  transfers between devices with their start and end apart: 12 -> 6, of which waited for: 4 -> 2; matrix products, arithmetic and copies ran while one was open for 23% -> 24% of each run, Pallas kernels for 34% -> 31%
where the time goes in v3:
time: 340 us; the launch traced here: 337 us
  Pallas kernels  157 us (46%)
  local copies, waits for them, and re-layouts  60.6 us (18%)
  matrix products  38.5 us (11%)
  waiting for transfers between devices  28.1 us (8%)
  blocking collectives  25.7 us (8%)
  between operations  15.2 us (4%)
  other arithmetic  11.3 us (3%)
    pallas_call x8, Pallas kernels, call(): pl.pallas_call(kernel, out_shape=out_shape, in_specs=[VMEM] * len(args),...  157 us
    all_gather x1, blocking collectives, on_device(): w_out = lax.all_gather(out_weight, row_axes, axis=0, tiled=True)  25.7 us
    dot_general x8, matrix products, contract(): lax.dot_general(left, right, (((left_axis,), (right_axis,)), ((), ())), p...  19.6 us
    reduce_scatter x3, waiting for transfers between devices, reduce_a(): lax.psum_scatter(values.astype(BF16), axes, scatter_dimension=0, tiled=True)  16.3 us
    reshape x2, local copies, waits for them, and re-layouts, on_device(): grad_context.astype(BF16).reshape(blocks, rows, heads_here, HEAD)  12.8 us
    reduce_scatter x1, waiting for transfers between devices, scatter_group(): lax.psum_scatter(values.astype(BF16), G_AXES, scatter_dimension=0, tiled=...  11.7 us
    unnamed x87, local copies, waits for them, and re-layouts  7.56 us
    convert_element_type x3, local copies, waits for them, and re-layouts, on_device(): share_fc.transpose(2, 3, 1, 0, 4).reshape(depth, hidden).astype(F32)  7.35 us
  transfers between devices with their start and end apart: 6, of which 2 were waited for; matrix products, arithmetic and copies ran while one was open for 24% of the time, Pallas kernels for 31%

profile of v3, /device:TPU:0, one launch (start us, length us, event | category | flops | bytes accessed | tf_op | source)
XLA Modules:
  0.0 336.7 jit_solution(11842569167293932254)
XLA Ops:
  11.9 21.2 %shard_map.271 = (f32[16,6,128]{2,1,0:T(8,128)S(1)}, f32[8,1,128]{2,1,0:T(1,128)S(1)}, bf16[16,64,384]{2,1,0:T(8,128)(2,1)S(1)}, bf16[4,64,512]{2,1,0:T(8,128)(2,1)S(1)}) custom-call(f32[6,128]{1,0:T(8,128)S(1)} %bitcast_convert_fusion.1.p_ref, f32[1,128]{1,0:T(1,128)S(1)} %convert_element_type.120.s_ref, bf16[4,64,384]{2,1,0:T(8,128)(2,1)S(1)} %reshape.293.q_ref, ...), custom_call_target="tpu_custom_call" | custom-call | bytes 33554432 | tf_op jit(solution)/shard_map/pallas_call | solution.py:165
  35.2 18.3 %shard_map.272 = bf16[8,128,1024]{2,1,0:T(8,128)(2,1)S(1)} custom-call(bf16[128,1024]{1,0:T(8,128)(2,1)S(1)} %add_convert_fusion.2.x_ref), custom_call_target="tpu_custom_call" | custom-call | bytes 33554432 | tf_op jit(solution)/shard_map/pallas_call | solution.py:165
  53.7 2.1 add_convert_fusion
  55.8 4.0 %reshape.330 = bf16[8,128,3,2,64]{4,3,2,1,0:T(2,128)(2,1)} reshape(bf16[1024,384]{1,0:T(8,128)(2,1)} %add_convert_fusion) | data formatting | bytes 1572864 | tf_op jit(solution)/shard_map/reshape | solution.py:506
  59.8 2.7 fusion.55
  64.9 25.7 %all_gather.12 = bf16[256,1024]{1,0:T(8,128)(2,1)S(1)} all-gather(bf16[64,1024]{1,0:T(8,128)(2,1)S(1)} %copy-done.25), channel_id=1, replica_groups=mesh['a'=4,'b1'=2,'b0'=2,'u'=1,'v'=2] {'a'}, dimensions={0}, use_global_device_ids=true | all-gather | bytes 655360 | tf_op jit(solution)/shard_map/all_gather | solution.py:483
  91.4 16.2 %shard_map.273 = f32[128,1024]{1,0:T(8,128)S(1)} custom-call(bf16[8,128,1024]{2,1,0:T(8,128)(2,1)S(1)} %bitcast.155), custom_call_target="tpu_custom_call" | custom-call | bytes 33554432 | tf_op jit(solution)/shard_map/pallas_call | solution.py:165
  109.4 19.0 %shard_map.274 = bf16[8,128,1024]{2,1,0:T(8,128)(2,1)S(1)} custom-call(bf16[128,1024]{1,0:T(8,128)(2,1)S(1)} %add_convert_fusion.1.x_ref), custom_call_target="tpu_custom_call" | custom-call | bytes 33554432 | tf_op jit(solution)/shard_map/pallas_call | solution.py:165
  128.5 3.0 fusion.54
  131.5 2.2 reshape.303
  133.8 2.6 fusion.65
  137.7 2.8 convolution_convert_fusion.2
  140.8 4.6 %convolution_convert_fusion.4 = bf16[512,1024]{1,0:T(8,128)(2,1)} fusion(bf16[1024,1024]{1,0:T(8,128)(2,1)} %all-gather.4.cloned.1.call-done, f32[1024,512]{1,0:T(8,128)} %copy-done.38, f32[512]{0:T(512)S(1)} %bitcast.197), kind=kOutput, calls=%fused_computation.15 | convolution fusion | flops 1079508992 | bytes 5244928 | tf_op jit(solution)/shard_map/dot_general | solution.py:59
  145.5 5.0 %fusion.64 = (f32[512]{0:T(512)S(1)}, bf16[1024,512]{1,0:T(8,128)(2,1)S(1)}) fusion(f32[1024,512]{1,0:T(8,128)} %copy-done.38, f32[512]{0:T(512)S(1)} %bitcast.198, bf16[512,1024]{1,0:T(8,128)(2,1)} %bitcast.179, bf16[1024,1024]{1,0:T(8,128)(2,1)} %all-gather.4.cloned.1.call-done), kind=kOutput, calls=%fused_computation.127 | convolution fusion | flops 1084751360 | bytes 6295552 | tf_op jit(solution)/shard_map/dot_general | solution.py:59
  151.8 19.1 %shard_map.275 = f32[128,1024]{1,0:T(8,128)S(1)} custom-call(bf16[8,128,1024]{2,1,0:T(8,128)(2,1)S(1)} %bitcast.156), custom_call_target="tpu_custom_call" | custom-call | bytes 33554432 | tf_op jit(solution)/shard_map/pallas_call | solution.py:165
  171.4 3.5 %convolution_convert_fusion.5 = bf16[1024,512]{1,0:T(8,128)(2,1)} fusion(bf16[1024,1024]{1,0:T(8,128)(2,1)S(1)} %bitcast.161, bf16[1024,512]{1,0:T(8,128)(2,1)} %copy-done.39), kind=kOutput, calls=%fused_computation.16 | convolution fusion | flops 1074266112 | bytes 4194304 | tf_op jit(solution)/shard_map/dot_general | solution.py:59
  175.0 11.7 %reduce-scatter.5.cloned.1.call-done = bf16[128,1024]{1,0:T(8,128)(2,1)} async-done(((bf16[1024,1024]{1,0:T(8,128)(2,1)}), bf16[128,1024]{1,0:T(8,128)(2,1)}) %reduce-scatter.5.cloned.1.call-update) | async-done | bytes 262160 | tf_op jit(solution)/shard_map/reduce_scatter | solution.py:73
  186.6 2.3 fusion.52
  189.8 16.6 %shard_map.276 = bf16[8,128,1024]{2,1,0:T(8,128)(2,1)S(1)} custom-call(bf16[128,1024]{1,0:T(8,128)(2,1)S(1)} %convert_element_type.135.x_ref), custom_call_target="tpu_custom_call" | custom-call | bytes 33554432 | tf_op jit(solution)/shard_map/pallas_call | solution.py:165
  207.8 2.0 reshape.331
  209.8 10.8 %copy.61 = bf16[8,128,2,64]{1,3,2,0:T(8,128)(2,1)S(1)} copy(bf16[8,128,2,64]{3,2,1,0:T(2,128)(2,1)} %reshape.331) | data formatting | bytes 524288 | tf_op jit(solution)/shard_map/reshape | solution.py:553
  224.7 3.0 fusion.14
  228.5 3.9 %fusion.57 = (f32[2,64]{1,0:T(2,128)S(1)}, bf16[8,128,2,64]{1,3,2,0:T(8,128)(2,1)}) fusion(f32[8,2,128,128]{2,3,1,0:T(8,128)} %fusion.34, f32[8,2,128,128]{2,3,1,0:T(8,128)} %copy-done.10, f32[8,2,128]{2,1,0:T(2,128)S(1)} %bitcast.186, bf16[8,128,1,2,64]{1,4,3,0,2:T(8,128)(2,1)} %copy-done.20), kind=kOutput, calls=%fused_computation.122 | convolution fusion | flops 35653632 | bytes 2630144 | tf_op jit(solution)/shard_map/nhqk,nkhd->nqhd/dot_general | solution.py:558
  236.9 16.5 %shard_map.277 = f32[128,1024]{1,0:T(8,128)S(1)} custom-call(bf16[8,128,1024]{2,1,0:T(8,128)(2,1)S(1)} %bitcast.157), custom_call_target="tpu_custom_call" | custom-call | bytes 33554432 | tf_op jit(solution)/shard_map/pallas_call | solution.py:165
  257.3 2.3 multiply_add_fusion.1
  260.9 16.2 %reduce-scatter.11.cloned.1.call-done.o_ref = bf16[64,1024]{1,0:T(8,128)(2,1)} async-done(((bf16[256,1024]{1,0:T(8,128)(2,1)}), bf16[64,1024]{1,0:T(8,128)(2,1)}) %reduce-scatter.11.cloned.1.call-update) | async-done | bytes 131088 | tf_op jit(solution)/shard_map/reduce_scatter | solution.py:540
  280.0 30.2 %shard_map.278 = (f32[6,128]{1,0:T(8,128)S(1)}, f32[2,4,64,384]{3,2,1,0:T(8,128)S(1)}, bf16[8,64,512]{2,1,0:T(8,128)(2,1)S(1)}, bf16[2,128,1024]{2,1,0:T(8,128)(2,1)S(1)}, bf16[2,64,1024]{2,1,0:T(8,128)(2,1)S(1)}) custom-call(f32[16,6,128]{2,1,0:T(8,128)S(1)} %reshape.319.x_ref, bf16[16,64,384]{2,1,0:T(8,128)(2,1)S(1)} %bitcast.162, ...), custom_call_target="tpu_custom_call" | custom-call | bytes 33554432 | tf_op jit(solution)/shard_map/pallas_call | solution.py:165
  310.2 2.1 reshape.323
  312.4 3.6 %copy.70 = f32[64,3,1,2,2,4,64]{6,5,4,3,1,0,2:T(4,128)} copy(f32[64,3,1,2,2,4,64]{6,4,1,0,5,3,2:T(2,128)} %bitcast.169) | data formatting | bytes 1572864 | tf_op jit(solution)/shard_map/transpose | solution.py:605
  315.9 3.4 %reshape.324 = f32[64,3072]{1,0:T(8,128)} reshape(f32[64,3,1,2,2,4,64]{6,5,4,3,1,0,2:T(4,128)} %copy.70) | data formatting | bytes 1572864 | tf_op jit(solution)/shard_map/reshape | solution.py:605
  320.6 3.0 copy.71
  323.7 3.0 reshape.326
  (191 shorter events, 38.9 us)
Async XLA Ops:
  7.2 26.1 %copy-start = (bf16[256,1024]{1,0:T(8,128)(2,1)S(1)}, bf16[256,1024]{1,0:T(8,128)(2,1)}, u32[]{:S(2)}) copy-start(bf16[256,1024]{1,0:T(8,128)(2,1)} %param.30) | copy-start | bytes 1572868
  7.2 121.3 %all-gather.6.cloned.1.call-start = ((), (), s32[]{:S(2)}) async-start(), calls=%async_computation.9 | async-start | bytes 2621440 | tf_op jit(solution)/shard_map/all_gather | solution.py:488
  8.8 1.7 copy-start.24
  10.0 1.7 copy-start.28
  10.0 1.7 copy-start.29
  10.1 1.7 copy-start.30
  10.1 1.7 copy-start.31
  10.1 1.7 copy-start.32
  10.1 1.7 copy-start.33
  10.1 1.8 copy-start.37
  11.6 23.1 %copy-start.8 = (f32[128,1024]{1,0:T(8,128)S(1)}, f32[128,1024]{1,0:T(8,128)}, u32[]{:S(2)}) copy-start(f32[128,1024]{1,0:T(8,128)} %param.16) | copy-start | bytes 1572868
  33.2 20.5 %copy-start.6 = (bf16[16,64,384]{2,1,0:T(8,128)(2,1)}, bf16[16,64,384]{2,1,0:T(8,128)(2,1)S(1)}, u32[]{:S(2)}) copy-start(bf16[16,64,384]{2,1,0:T(8,128)(2,1)S(1)} %get-tuple-element.25) | copy-start | bytes 2359300
  34.2 106.6 %all-gather.4.cloned.1.call-start = ((), (), s32[]{:S(2)}) async-start(), calls=%async_computation.5 | async-start | bytes 2359296 | tf_op jit(solution)/shard_map/all_gather | solution.py:69
  53.6 2.2 copy-start.1
  64.2 26.4 %copy-start.10 = (f32[8,2,128,128]{2,3,1,0:T(8,128)}, f32[8,2,128,128]{2,3,1,0:T(8,128)S(1)}, u32[]{:S(2)}) copy-start(f32[8,2,128,128]{2,3,1,0:T(8,128)S(1)} %get-tuple-element.76) | copy-start | bytes 3145732
  64.9 26.5 %copy-start.14 = (bf16[8,128,2,64]{1,0,3,2:T(8,128)(2,1)}, bf16[8,128,2,64]{1,0,3,2:T(8,128)(2,1)S(1)}, u32[]{:S(2)}) copy-start(bf16[8,128,2,64]{1,0,3,2:T(8,128)(2,1)S(1)} %copy.58) | copy-start | bytes 786436
  90.6 16.9 %copy-start.17 = (bf16[256,1024]{1,0:T(8,128)(2,1)}, bf16[256,1024]{1,0:T(8,128)(2,1)S(1)}, u32[]{:S(2)}) copy-start(bf16[256,1024]{1,0:T(8,128)(2,1)S(1)} %all_gather.12) | copy-start | bytes 1572868
  90.6 17.0 %copy-start.9 = (f32[128,1024]{1,0:T(8,128)S(1)}, f32[128,1024]{1,0:T(8,128)}, u32[]{:S(2)}) copy-start(f32[128,1024]{1,0:T(8,128)} %param.16) | copy-start | bytes 1572868
  90.6 17.0 %copy-start.16 = (f32[128,1024]{1,0:T(8,128)S(1)}, f32[128,1024]{1,0:T(8,128)}, u32[]{:S(2)}) copy-start(f32[128,1024]{1,0:T(8,128)} %param.18) | copy-start | bytes 1572868
  108.5 78.2 %reduce-scatter.5.cloned.1.call-start = ((), (), s32[]{:S(2)}) async-start(), calls=%async_computation.4 | async-start | bytes 2359296 | tf_op jit(solution)/shard_map/reduce_scatter | solution.py:73
  133.7 3.9 %copy-start.23 = (bf16[4,128,1024]{2,1,0:T(8,128)(2,1)S(1)}, bf16[4,128,1024]{2,1,0:T(8,128)(2,1)}, u32[]{:S(2)}) copy-start(bf16[4,128,1024]{2,1,0:T(8,128)(2,1)} %get-tuple-element.46) | copy-start | bytes 3145732
  140.5 120.4 %reduce-scatter.9.cloned.1.call-start = ((), (), s32[]{:S(2)}) async-start(), calls=%async_computation.7 | async-start | bytes 1310720 | tf_op jit(solution)/shard_map/reduce_scatter | solution.py:540
  145.4 115.5 %reduce-scatter.7.cloned.1.call-start = ((), (), s32[]{:S(2)}) async-start(), calls=%async_computation.6 | async-start | bytes 1310720 | tf_op jit(solution)/shard_map/reduce_scatter | solution.py:540
  145.4 5.1 %copy-start.19 = (bf16[1024,512]{1,0:T(8,128)(2,1)S(1)}, bf16[1024,512]{1,0:T(8,128)(2,1)}, u32[]{:S(2)}) copy-start(bf16[1024,512]{1,0:T(8,128)(2,1)} %reshape.303) | copy-start | bytes 3145732
  151.8 19.1 %copy-start.12 = (f32[128,1024]{1,0:T(8,128)S(1)}, f32[128,1024]{1,0:T(8,128)}, u32[]{:S(2)}) copy-start(f32[128,1024]{1,0:T(8,128)} %copy-done.11) | copy-start | bytes 1572868
  174.9 102.3 %reduce-scatter.11.cloned.1.call-start = ((), (), s32[]{:S(2)}) async-start(), calls=%async_computation.8 | async-start | bytes 655360 | tf_op jit(solution)/shard_map/reduce_scatter | solution.py:540
  188.9 17.5 %copy-start.18 = (bf16[256,1024]{1,0:T(8,128)(2,1)S(1)}, bf16[256,1024]{1,0:T(8,128)(2,1)}, u32[]{:S(2)}) copy-start(bf16[256,1024]{1,0:T(8,128)(2,1)} %copy-done.17) | copy-start | bytes 1572868
  209.8 14.8 %copy-start.22 = (bf16[8,128,1,2,64]{1,4,3,0,2:T(8,128)(2,1)S(1)}, bf16[8,128,1,2,64]{1,4,3,0,2:T(8,128)(2,1)}, u32[]{:S(2)}) copy-start(bf16[8,128,1,2,64]{1,4,3,0,2:T(8,128)(2,1)} %copy-done.21) | copy-start | bytes 786436
  228.5 7.0 %copy-start.7 = (bf16[16,64,384]{2,1,0:T(8,128)(2,1)S(1)}, bf16[16,64,384]{2,1,0:T(8,128)(2,1)}, u32[]{:S(2)}) copy-start(bf16[16,64,384]{2,1,0:T(8,128)(2,1)} %copy-done.6) | copy-start | bytes 2359300
  236.9 17.3 %copy-start.15 = (bf16[8,128,2,64]{1,0,3,2:T(8,128)(2,1)S(1)}, bf16[8,128,2,64]{1,0,3,2:T(8,128)(2,1)}, u32[]{:S(2)}) copy-start(bf16[8,128,2,64]{1,0,3,2:T(8,128)(2,1)} %copy-done.14) | copy-start | bytes 786436
  255.4 4.2 %copy-start.2 = (bf16[8,128,1024]{2,1,0:T(8,128)(2,1)S(1)}, bf16[8,128,1024]{2,1,0:T(8,128)(2,1)}, u32[]{:S(2)}) copy-start(bf16[8,128,1024]{2,1,0:T(8,128)(2,1)} %copy-done.1) | copy-start | bytes 6291460
  257.2 2.3 copy-start.27
  (14 other events, 17.6 us)
Sparse Core Ops, SparseCore 0:
  34.4 59.2 all-gather.5
  108.6 31.0 all-gather.3
  143.0 43.6 reduce-scatter.4
  188.9 27.1 reduce-scatter.8
  218.8 25.7 reduce-scatter.6
  255.5 21.5 reduce-scatter.10
